TPU v7x, 32 devices: a whole 2x2x4 slice. The times are simulated.
32 devices in a mesh: batch: 4 (over x, core), seq: 8 (over z, y).
Axes of the slice: x: 2, y: 2, z: 4, core: 2. Of those that a mesh axis runs over, the one named last changes fastest.
Arguments:
- inputs: float32 [8, 2048, 512], P('batch', 'seq'), may hold values from -12 to 12
- norm_gain: float32 [512], replicated, may hold values from 0.25 to 1.75
- norm_bias: float32 [512], replicated, may hold values from -3 to 3
- query_weight: float32 [512, 512], replicated, may hold values from -0.25 to 0.25
- query_bias: float32 [512], replicated, may hold values from -3 to 3
- key_weight: float32 [512, 512], replicated, may hold values from -0.25 to 0.25
- value_weight: float32 [512, 512], replicated, may hold values from -0.25 to 0.25
- value_bias: float32 [512], replicated, may hold values from -3 to 3
- mixer_weight: float32 [512, 512], replicated, may hold values from -0.5 to 0.5
- mixer_bias: float32 [512], replicated, may hold values from -3 to 3
- final_gain: float32 [512], replicated, may hold values from 0.25 to 1.75
- final_bias: float32 [512], replicated, may hold values from -3 to 3
- inner_weight: float32 [512, 2048], replicated, may hold values from -0.25 to 0.25
- inner_bias: float32 [2048], replicated, may hold values from -3 to 3
- outer_weight: float32 [2048, 512], replicated, may hold values from -0.125 to 0.125
- outer_bias: float32 [512], replicated, may hold values from -3 to 3
- cotangent: float32 [8, 2048, 512], P('batch', 'seq'), may hold values from -6 to 6
Outputs:
- outputs: float32 [8, 2048, 512], P('batch', 'seq')
- inputs_grad: float32 [8, 2048, 512], P('batch', 'seq')
- norm_gain_grad: float32 [512], replicated
- norm_bias_grad: float32 [512], replicated
- query_weight_grad: float32 [512, 512], replicated
- query_bias_grad: float32 [512], replicated
- key_weight_grad: float32 [512, 512], replicated
- value_weight_grad: float32 [512, 512], replicated
- value_bias_grad: float32 [512], replicated
- mixer_weight_grad: float32 [512, 512], replicated
- mixer_bias_grad: float32 [512], replicated
- final_gain_grad: float32 [512], replicated
- final_bias_grad: float32 [512], replicated
- inner_weight_grad: float32 [512, 2048], replicated
- inner_bias_grad: float32 [2048], replicated
- outer_weight_grad: float32 [2048, 512], replicated
- outer_bias_grad: float32 [512], replicated
All inputs are finite; a program needn't handle non-finite values.
Results may differ from a plain program's by a relative error of at most 0.0003.
Values sent between devices are 32-bit elements; how exact they have to be, the bound alone decides.
No kernel may reach another device: no remote copies, remote signals or barrier semaphores. Data moves between devices by JAX's collectives and lax.ppermute only.
A program may use at most 192 MiB of HBM per device.

v0:
```python
import functools
import math
import types

import jax
import jax.numpy as jnp
import numpy as np
from jax import lax
from jax.experimental import pallas as pl
from jax.experimental.pallas import tpu as pltpu
from jax.sharding import PartitionSpec as P

HEADS = 8
BLOCK = 16
LOG2E = 1.4426950408889634
LN2 = 0.6931471805599453
ROOT_HALF = 0.7071067811865476
INV_ROOT_TWO_PI = 0.3989422804014327
EPS = 1e-06
FAR = -1e30
SPARE = 16
TOKEN = (8, 128)
PLAN = (
    "first_norm", "project_qk", "project_v", "coarser", "rest_coarser", "local", "remote",
    "outer0", "outer1", "inner0", "A", "inner1", "middle_grad", "B", "A", "pairs0", "pairs1", "A",
    "rows_grad", "B", "A", "finer", "square0", "finer", "B", "C", "square1", "A", "C", "A", "B",
    "C", "first_grad", "D", "A", "C", "B", "D", "D", "C", "B", "D", "A", "C", "D", "B", "D", "C",
    "B", "D", "write_inner", "write_outer", "C", "D", "write_square0", "write_square1",
)
COST = 10**10
INNER, OUTER, ODD, FIRST, LAST, CORE = range(6)

bf16 = jnp.bfloat16
f32 = jnp.float32
VMEM = pl.BlockSpec(memory_space=pltpu.VMEM)
ANY = pl.BlockSpec(memory_space=pl.ANY)
HBM = pl.BlockSpec(memory_space=pltpu.MemorySpace.HBM)


def split(value):
    high = value.astype(bf16)
    return high, (value - high.astype(f32)).astype(bf16)


def dg(left, right, left_dim=1, right_dim=0):
    return lax.dot_general(
        left, right, (((left_dim,), (right_dim,)), ((), ())), preferred_element_type=f32
    )


def dot3(left, right, left_dim=1, right_dim=0):
    return (
        dg(left[0], right[0], left_dim, right_dim)
        + dg(left[0], right[1], left_dim, right_dim)
        + dg(left[1], right[0], left_dim, right_dim)
    )


def dot2(left, exact, left_dim=1, right_dim=0):
    return dg(left[0], exact, left_dim, right_dim) + dg(left[1], exact, left_dim, right_dim)


def exact_dot2(exact, right, left_dim=1, right_dim=0):
    return dg(exact, right[0], left_dim, right_dim) + dg(exact, right[1], left_dim, right_dim)


def two_diagonal(pair_rows):
    half = pair_rows.shape[0] // 2
    zero = jnp.zeros((half, pair_rows.shape[1]), pair_rows.dtype)
    return jnp.concatenate(
        [
            jnp.concatenate([pair_rows[:half], zero], axis=1),
            jnp.concatenate([zero, pair_rows[half:]], axis=1),
        ],
        axis=0,
    )


def two_masked(pair_lanes):
    half = pair_lanes.shape[1] // 2
    lower = lax.broadcasted_iota(jnp.int32, pair_lanes.shape, 1) < half
    wide = pair_lanes.astype(f32)
    return jnp.concatenate(
        [jnp.where(lower, wide, 0.0), jnp.where(lower, 0.0, wide)], axis=0
    ).astype(bf16)


def take_diagonal(product):
    half, width = product.shape[0] // 2, product.shape[1] // 2
    return jnp.concatenate([product[:half, :width], product[half:, width:]], axis=0)


def pair_weights(keys, queries_t, bias):
    diag_high, diag_low = two_diagonal(queries_t[0]), two_diagonal(queries_t[1])
    scores = dg(
        jnp.concatenate([keys[0], keys[1], keys[0]], axis=1),
        jnp.concatenate([diag_high, diag_high, diag_low], axis=0),
    )
    return jnp.exp2(scores + bias)


def tile_forward(keys, values_t, queries_t, bias):
    weights = pair_weights(keys, queries_t, bias)
    denominator = jnp.sum(weights, axis=0, keepdims=True)
    high, low = split(weights)
    wide = dg(jnp.concatenate([values_t[0], values_t[1]], axis=0), high)
    size = values_t[0].shape[0]
    product = wide[:size] + wide[size:] + dg(values_t[0], low)
    width = denominator.shape[1] // 2
    return (
        take_diagonal(product),
        jnp.concatenate([denominator[:, :width], denominator[:, width:]], axis=0),
    )


def tile_backward(keys, keys_t, values, queries_t, queries_m, grads_t, grads_m, grad_den, bias):
    weights = pair_weights(keys, queries_t, bias)
    diag_high, diag_low = two_diagonal(grads_t[0]), two_diagonal(grads_t[1])
    grad_weights = (
        dg(
            jnp.concatenate([values[0], values[1], values[0]], axis=1),
            jnp.concatenate([diag_high, diag_high, diag_low], axis=0),
        )
        + grad_den
    )
    scores = split(weights * grad_weights)
    weights = split(weights)

    def gather(pairs, masked):
        wide = dg(pairs[0], jnp.concatenate([masked[0], masked[1]], axis=1))
        half = wide.shape[1] // 2
        return wide[:, :half] + wide[:, half:] + dg(pairs[1], masked[0])

    grad_values = gather(weights, grads_m)
    grad_keys = gather(scores, queries_m)
    wide = dg(jnp.concatenate([keys_t[0], keys_t[1]], axis=0), scores[0])
    size = keys_t[0].shape[0]
    product = wide[:size] + wide[size:] + dg(keys_t[0], scores[1])
    return take_diagonal(product), grad_keys, grad_values


def lanes(parts, start, size):
    return tuple(part[:, start : start + size] for part in parts)


def rows(parts, start, size):
    return tuple(part[start : start + size] for part in parts)


def block_of(parts, row, row_size, lane, lane_size):
    return tuple(part[row : row + row_size, lane : lane + lane_size] for part in parts)


def stack(first, second):
    return tuple(jnp.concatenate([one, two], axis=0) for one, two in zip(first, second))


def norm_rows(values):
    center = values - jnp.mean(values, axis=-1, keepdims=True)
    inverse = lax.rsqrt(jnp.mean(center * center, axis=-1, keepdims=True) + EPS)
    return center * inverse, inverse


def norm_grad(grad_rows, unit_rows, inverse, gain):
    grad_unit = grad_rows * gain
    return inverse * (
        grad_unit
        - jnp.mean(grad_unit, axis=-1, keepdims=True)
        - unit_rows * jnp.mean(grad_unit * unit_rows, axis=-1, keepdims=True)
    )


def first_norm_kernel(groups, span, place_ref, x_ref, unit_ref, inv_ref, inner_ref, outer_ref):
    width = x_ref.shape[-1]
    for group in range(groups):
        own = slice(group * span, (group + 1) * span)
        unit, inverse = norm_rows(x_ref[own, :])
        unit_ref[own, :] = unit
        inv_ref[own, :] = inverse
        runs = span // BLOCK
        inner_ref[group, BLOCK:, :] = jnp.mean(unit.reshape(BLOCK, runs, width), axis=1)
        inner_start = pl.multiple_of(group * span + place_ref[INNER], BLOCK)
        outer_start = pl.multiple_of(group * span + place_ref[OUTER], BLOCK)
        inner_ref[group, :BLOCK, :] = unit_ref[pl.ds(inner_start, BLOCK), :]
        outer_ref[group] = unit_ref[pl.ds(outer_start, BLOCK), :]


def project_kernel(groups, span, scales, unit_ref, gain_ref, shift_ref, mean_ref, *refs):
    count = len(scales)
    weights, refs = refs[:count], refs[count:]
    biased = [scale is not None for scale in scales]
    biases, outs = list(refs[: sum(biased)]), refs[sum(biased) :]
    normed = split(unit_ref[...] * gain_ref[...] + shift_ref[...])
    means = mean_ref[...]
    coarse = means.shape[0]
    for index, (weight, scale) in enumerate(zip(weights, scales)):
        result = dot3(normed, split(weight[...]))
        if scale is not None:
            result = result + biases.pop(0)[...]
            if scale != 1.0:
                result = result * scale
        outs[2 * index][...] = result
        for group in range(groups):
            part = split(result[group * span : (group + 1) * span])
            outs[2 * index + 1][group * coarse : (group + 1) * coarse, :] = exact_dot2(means, part)


def fill_bias(bias_ref, near_ref, place_ref):
    rows_total = near_ref.shape[0]
    bias_ref[0] = near_ref[...]
    bias_ref[1] = near_ref[...]
    before = place_ref[FIRST].astype(f32) * FAR
    after = place_ref[LAST].astype(f32) * FAR
    bias_ref[0, :BLOCK, :] = near_ref[:BLOCK, :] + before
    bias_ref[1, rows_total - BLOCK :, :] = near_ref[rows_total - BLOCK :, :] + after


def local_kernel(
    groups, span, place_ref, q_ref, k_ref, v_ref, qc_ref, kc_ref, vc_ref, inner_ref, outer_ref,
    gain_ref, shift_ref, kw_ref, vw_ref, vb_ref, near_ref, one_ref,
    num_ref, den_ref, numc_ref, denc_ref, halo_ref, hk_ref, hv_ref, bias_ref,
):
    width = q_ref.shape[-1]
    half = span // 2
    coarse = qc_ref.shape[0] // groups
    pairs = HEADS // 2
    pair_width = width // pairs
    tile_keys = half + 2 * BLOCK
    fill_bias(bias_ref, near_ref, place_ref)
    odd = place_ref[ODD].astype(f32)
    for group in range(groups):
        inner, outer = inner_ref[group, :BLOCK, :], outer_ref[group]
        at = group * 2 * BLOCK
        halo_ref[at : at + BLOCK, :] = inner * odd + outer * (1.0 - odd)
        halo_ref[at + BLOCK : at + 2 * BLOCK, :] = inner * (1.0 - odd) + outer * odd
    normed = split(halo_ref[...] * gain_ref[...] + shift_ref[...])
    halo_keys = dot3(normed, split(kw_ref[...]))
    halo_values = dot3(normed, split(vw_ref[...])) + vb_ref[...]
    hk_ref[...] = halo_keys
    hv_ref[...] = halo_values
    for group in range(groups):
        own = slice(group * span, (group + 1) * span)
        left = slice(group * 2 * BLOCK, group * 2 * BLOCK + BLOCK)
        right = slice(group * 2 * BLOCK + BLOCK, (group + 1) * 2 * BLOCK)
        own_c = slice(group * coarse, group * coarse + half)
        keys = split(jnp.concatenate([halo_keys[left], k_ref[own, :], halo_keys[right]], axis=0))
        values = jnp.concatenate([halo_values[left], v_ref[own, :], halo_values[right]], axis=0)
        values_t = split(values.T)
        queries_t = split(q_ref[own, :].T)
        keys_c = split(kc_ref[own_c, :])
        values_ct = split(vc_ref[own_c, :].T)
        queries_ct = split(qc_ref[own_c, :].T)
        for pair in range(pairs):
            at = pair * pair_width
            out = slice(group * width + at, group * width + at + pair_width)
            heads = slice((group * pairs + pair) * 2, (group * pairs + pair) * 2 + 2)
            for tile in range(2):
                num, den = tile_forward(
                    block_of(keys, tile * half, tile_keys, at, pair_width),
                    block_of(values_t, at, pair_width, tile * half, tile_keys),
                    block_of(queries_t, at, pair_width, tile * half, half),
                    bias_ref[tile],
                )
                num_ref[out, tile * half : (tile + 1) * half] = num
                den_ref[heads, tile * half : (tile + 1) * half] = den
            num, den = tile_forward(
                lanes(keys_c, at, pair_width),
                rows(values_ct, at, pair_width),
                rows(queries_ct, at, pair_width),
                one_ref[...],
            )
            numc_ref[out, :] = num
            denc_ref[heads, :] = den


def remote_kernel(
    groups, span, crossing, *refs
):
    far_parts, refs = refs[:crossing], refs[crossing:]
    (
        x_ref, num_ref, den_ref, numc_ref, denc_ref, qc_ref, kc_ref, vc_ref, gain_ref, shift_ref,
        kw_ref, vw_ref, vb_ref, rest_ref, expand_ref, mw_ref, mb_ref, fgain_ref, fshift_ref, ob_ref,
        cot_ref,
        far_ref, rk_ref, rv_ref, mixed_ref, rden_ref, unit_ref, inv_ref, acc_ref, fhigh_ref, flow_ref,
        chigh_ref, clow_ref, mid_ref,
    ) = refs
    width = x_ref.shape[-1]
    half = span // 2
    coarse = qc_ref.shape[0] // groups
    far = far_ref.shape[0] // groups
    pairs = HEADS // 2
    pair_width = width // pairs
    head_width = width // HEADS
    local_rest = rest_ref.shape[0] - far
    for group in range(groups):
        for level, part in enumerate(far_parts):
            at = group * far + level * BLOCK
            far_ref[at : at + BLOCK, :] = part[group, part.shape[1] - BLOCK :, :]
    normed = split(far_ref[...] * gain_ref[...] + shift_ref[...])
    far_keys = dot3(normed, split(kw_ref[...]))
    far_values = dot3(normed, split(vw_ref[...])) + vb_ref[...]
    rk_ref[...] = far_keys
    rv_ref[...] = far_values
    expand = expand_ref[...]
    for group in range(groups):
        rest = slice(group * coarse + half, group * coarse + half + local_rest)
        remote = slice(group * far, (group + 1) * far)
        keys = split(jnp.concatenate([kc_ref[rest, :], far_keys[remote]], axis=0))
        values_t = split(jnp.concatenate([vc_ref[rest, :], far_values[remote]], axis=0).T)
        queries_t = split(qc_ref[group * coarse + half : (group + 1) * coarse, :].T)
        nums, dens = [], []
        for pair in range(pairs):
            at = pair * pair_width
            num, den = tile_forward(
                lanes(keys, at, pair_width),
                rows(values_t, at, pair_width),
                rows(queries_t, at, pair_width),
                rest_ref[...],
            )
            nums.append(num)
            dens.append(den)
        own_t = slice(group * width, (group + 1) * width)
        own_h = slice(group * HEADS, (group + 1) * HEADS)
        numc = jnp.concatenate([numc_ref[own_t, :], jnp.concatenate(nums, axis=0)], axis=1)
        denc = jnp.concatenate([denc_ref[own_h, :], jnp.concatenate(dens, axis=0)], axis=1)
        num = num_ref[own_t, :] + dot2(split(numc), expand)
        den = den_ref[own_h, :] + dot2(split(denc), expand)
        inverse = 1.0 / den
        rden_ref[own_h, :] = inverse
        spread = jnp.concatenate(
            [
                jnp.broadcast_to(inverse[head : head + 1], (head_width, span))
                for head in range(HEADS)
            ],
            axis=0,
        )
        mixed_t = num * spread
        own = slice(group * span, (group + 1) * span)
        mixed_ref[own_t, :] = mixed_t
        mid_ref[own, :] = mixed_t.T
    middle = x_ref[...] + dot3(split(mid_ref[...]), split(mw_ref[...])) + mb_ref[...]
    unit, inverse = norm_rows(middle)
    unit_ref[...] = unit
    inv_ref[...] = inverse
    fhigh_ref[...], flow_ref[...] = split(unit * fgain_ref[...] + fshift_ref[...])
    chigh_ref[...], clow_ref[...] = split(cot_ref[...])
    acc_ref[...] = middle + ob_ref[...]


def half_of(own, place_ref, size):
    side = place_ref[CORE] if own else 1 - place_ref[CORE]
    return pl.ds(pl.multiple_of(side * size, size), size)


def outer_kernel(
    own, place_ref, fhigh_ref, flow_ref, chigh_ref, clow_ref, iw_ref, ib_ref,
    joint_ref, hhigh_ref, hlow_ref, slope_ref,
):
    units = half_of(own, place_ref, slope_ref.shape[1])
    inner = dot3((fhigh_ref[...], flow_ref[...]), split(iw_ref[:, units])) + ib_ref[:, units]
    cumulative = 0.5 * (1.0 + lax.erf(inner * ROOT_HALF))
    hidden = split(inner * cumulative)
    slope_ref[...] = cumulative + inner * jnp.exp(-0.5 * inner * inner) * INV_ROOT_TWO_PI
    hhigh_ref[...], hlow_ref[...] = hidden
    joint_ref[...] = dot3(hidden, (chigh_ref[...], clow_ref[...]), 0, 0)


def inner_kernel(
    own, place_ref, fhigh_ref, flow_ref, chigh_ref, clow_ref, hhigh_ref, hlow_ref, slope_ref,
    iw_ref, ow_ref, acc_ref, *refs
):
    giw_ref, gib_ref, nacc_ref, ngacc_ref = refs[-4:]
    units = half_of(own, place_ref, slope_ref.shape[1])
    cot = chigh_ref[...], clow_ref[...]
    hidden = hhigh_ref[...], hlow_ref[...]
    iw, ow = split(iw_ref[:, units]), split(ow_ref[units, :])
    grad_inner = dot3(cot, ow, 1, 1) * slope_ref[...]
    gib_ref[...] = jnp.sum(grad_inner, axis=0, keepdims=True)
    grad_inner = split(grad_inner)
    giw = dot3((fhigh_ref[...], flow_ref[...]), grad_inner, 0, 0)
    width = giw.shape[0]
    giw_ref[:width, :] = giw[:, :width]
    giw_ref[width:, :] = giw[:, width:]
    nacc_ref[...] = acc_ref[...] + dot3(hidden, ow)
    grad_fnorm = dot3(grad_inner, iw, 1, 1)
    ngacc_ref[...] = refs[0][...] + grad_fnorm if own else grad_fnorm


def middle_grad_kernel(
    groups, span, cot_ref, gf_ref, unit_ref, inv_ref, fgain_ref, mixed_ref, rden_ref, mw_ref,
    expand_ref,
    gmid_ref, gmw_ref, vec_ref, gnum_ref, gnumt_ref, gden_ref, gnumct_ref, gdenc_ref,
):
    width = cot_ref.shape[-1]
    head_width = width // HEADS
    cot = cot_ref[...]
    gf = gf_ref[...]
    unit = unit_ref[...]
    gmid = cot + norm_grad(gf, unit, inv_ref[...], fgain_ref[...])
    gmid_ref[...] = gmid
    vec_ref[0:1, :] = jnp.sum(gf * unit, axis=0, keepdims=True)
    vec_ref[1:2, :] = jnp.sum(gf, axis=0, keepdims=True)
    vec_ref[2:3, :] = jnp.sum(gmid, axis=0, keepdims=True)
    vec_ref[3:4, :] = jnp.sum(cot, axis=0, keepdims=True)
    gmid = split(gmid)
    expand = expand_ref[...]
    grad_mixed = dot3(gmid, split(mw_ref[...]), 1, 1)
    total = None
    for group in range(groups):
        own = slice(group * span, (group + 1) * span)
        own_t = slice(group * width, (group + 1) * width)
        own_h = slice(group * HEADS, (group + 1) * HEADS)
        mixed_t = mixed_ref[own_t, :]
        part = dot3(split(mixed_t), rows(gmid, group * span, span))
        total = part if total is None else total + part
        grad_t = grad_mixed[own].T
        inverse = rden_ref[own_h, :]
        spread = jnp.concatenate(
            [
                jnp.broadcast_to(inverse[head : head + 1], (head_width, span))
                for head in range(HEADS)
            ],
            axis=0,
        )
        product = grad_t * mixed_t
        dens = jnp.concatenate(
            [
                jnp.sum(product[head * head_width : (head + 1) * head_width], axis=0, keepdims=True)
                for head in range(HEADS)
            ],
            axis=0,
        )
        gden = -dens * inverse
        gnum_t = grad_t * spread
        gnumt_ref[own_t, :] = gnum_t
        gnum_ref[own, :] = gnum_t.T
        gden_ref[own_h, :] = gden
        gnumct_ref[own_t, :] = dot2(split(gnum_t), expand, 1, 1)
        gdenc_ref[own_h, :] = dot2(split(gden), expand, 1, 1)
    gmw_ref[...] = total


def pairs_grad_kernel(
    groups, part, span, place_ref, q_ref, k_ref, v_ref, qc_ref, kc_ref, vc_ref, hk_ref, hv_ref,
    rk_ref, rv_ref, gnum_ref, gnumt_ref, gden_ref, gnumct_ref, gdenc_ref, near_ref, one_ref,
    rest_ref, mean_ref,
    dq_ref, dk_ref, dv_ref, odk_ref, odv_ref,
    bias_ref, dkx_ref, dvx_ref, dkc_ref, dvc_ref, dqt_ref, dqct_ref,
):
    full = q_ref.shape[-1]
    width = full // 2
    half = span // 2
    coarse = qc_ref.shape[0] // groups
    far = rk_ref.shape[0] // groups
    pairs = HEADS // 4
    pair_width = width // pairs
    tile_keys = half + 2 * BLOCK
    local_rest = rest_ref.shape[0] - far
    local_coarse = half + local_rest
    rest_keys = local_rest + far
    ours = slice(part * width, (part + 1) * width)
    fill_bias(bias_ref, near_ref, place_ref)
    means = mean_ref[...]
    zero = jnp.zeros((coarse - local_coarse, width), f32)
    for group in range(groups):
        fine = slice(group * span, (group + 1) * span)
        rough = slice(group * coarse, group * coarse + coarse)
        near_rough = slice(group * coarse, group * coarse + local_coarse)
        left = slice(group * 2 * BLOCK, group * 2 * BLOCK + BLOCK)
        right = slice(group * 2 * BLOCK + BLOCK, (group + 1) * 2 * BLOCK)
        remote = slice(group * far, (group + 1) * far)
        ours_t = slice(group * full + part * width, group * full + (part + 1) * width)
        keys_f = jnp.concatenate(
            [hk_ref[left, ours], k_ref[fine, ours], hk_ref[right, ours]], axis=0
        )
        keys, keys_t = split(keys_f), split(keys_f.T)
        values = split(
            jnp.concatenate([hv_ref[left, ours], v_ref[fine, ours], hv_ref[right, ours]], axis=0)
        )
        q = q_ref[fine, ours]
        queries, queries_t = split(q), split(q.T)
        grads, grads_t = split(gnum_ref[fine, ours]), split(gnumt_ref[ours_t, :])
        keys_cf = jnp.concatenate([kc_ref[near_rough, ours], rk_ref[remote, ours]], axis=0)
        keys_c, keys_ct = split(keys_cf), split(keys_cf.T)
        values_c = split(
            jnp.concatenate([vc_ref[near_rough, ours], rv_ref[remote, ours]], axis=0)
        )
        qc = qc_ref[rough, ours]
        queries_c, queries_ct = split(qc), split(qc.T)
        gnumct = gnumct_ref[ours_t, :]
        grads_c, grads_ct = split(gnumct.T), split(gnumct)
        for pair in range(pairs):
            at = pair * pair_width
            cols = slice(at, at + pair_width)
            head = group * HEADS + part * (HEADS // 2) + 2 * pair

            def den_rows(ref, start):
                both = ref[head : head + 2, start : start + half]
                return jnp.concatenate([both[0:1], both[1:2]], axis=1)

            def masked(parts, start):
                return tuple(
                    two_masked(value) for value in block_of(parts, start, half, at, pair_width)
                )

            for tile in range(2):
                start = tile * half
                dq, dk, dv = tile_backward(
                    block_of(keys, start, tile_keys, at, pair_width),
                    block_of(keys_t, at, pair_width, start, tile_keys),
                    block_of(values, start, tile_keys, at, pair_width),
                    block_of(queries_t, at, pair_width, start, half),
                    masked(queries, start),
                    block_of(grads_t, at, pair_width, start, half),
                    masked(grads, start),
                    den_rows(gden_ref, start),
                    bias_ref[tile],
                )
                dqt_ref[cols, start : start + half] = dq
                if tile == 0:
                    dkx_ref[:tile_keys, cols] = dk
                    dvx_ref[:tile_keys, cols] = dv
                else:
                    shared = slice(start, start + 2 * BLOCK)
                    fresh = slice(start + 2 * BLOCK, start + tile_keys)
                    dkx_ref[shared, cols] = dkx_ref[shared, cols] + dk[: 2 * BLOCK]
                    dvx_ref[shared, cols] = dvx_ref[shared, cols] + dv[: 2 * BLOCK]
                    dkx_ref[fresh, cols] = dk[2 * BLOCK :]
                    dvx_ref[fresh, cols] = dv[2 * BLOCK :]
            for start, count, bias in ((0, half, one_ref), (half, rest_keys, rest_ref)):
                dq, dk, dv = tile_backward(
                    block_of(keys_c, start, count, at, pair_width),
                    block_of(keys_ct, at, pair_width, start, count),
                    block_of(values_c, start, count, at, pair_width),
                    block_of(queries_ct, at, pair_width, start, half),
                    masked(queries_c, start),
                    block_of(grads_ct, at, pair_width, start, half),
                    masked(grads_c, start),
                    den_rows(gdenc_ref, start),
                    bias[...],
                )
                dqct_ref[cols, start : start + half] = dq
                dkc_ref[start : start + count, cols] = dk
                dvc_ref[start : start + count, cols] = dv
        distant = slice(
            groups * 2 * BLOCK + group * far, groups * 2 * BLOCK + (group + 1) * far
        )
        odk_ref[distant, :] = dkc_ref[local_coarse:, :] * LN2
        odv_ref[distant, :] = dvc_ref[local_coarse:, :]
        odk_ref[left, :] = dkx_ref[:BLOCK, :] * LN2
        odk_ref[right, :] = dkx_ref[span + BLOCK :, :] * LN2
        odv_ref[left, :] = dvx_ref[:BLOCK, :]
        odv_ref[right, :] = dvx_ref[span + BLOCK :, :]

        def spread(ref):
            local = jnp.concatenate([ref[:local_coarse, :], zero], axis=0)
            return exact_dot2(means, split(local), 0, 0)

        dk_ref[fine, :] = (dkx_ref[BLOCK : span + BLOCK, :] + spread(dkc_ref)) * LN2
        dv_ref[fine, :] = dvx_ref[BLOCK : span + BLOCK, :] + spread(dvc_ref)
        dq_ref[fine, :] = (dqt_ref[...] + dot2(split(dqct_ref[...]), means)).T


def square_grad_kernel(
    part, scale, place_ref, unit_ref, halo_ref, far_ref, gain_ref, shift_ref, gmw_ref,
    dq_ref, dk_ref, dv_ref, odk_ref, odv_ref, own_ref, send_ref, full_ref,
):
    width = unit_ref.shape[-1]
    half = width // 2
    core = place_ref[CORE]
    mine = pl.ds(pl.multiple_of(core * half, half), half)
    other = pl.ds(pl.multiple_of((1 - core) * half, half), half)
    outside = jnp.concatenate([halo_ref[...], far_ref[...]], axis=0)
    normed = split(unit_ref[...] * gain_ref[...] + shift_ref[...])
    normed_out = split(outside * gain_ref[...] + shift_ref[...])
    full_ref[0] = dot3(normed, split(dq_ref[...] * scale), 0, 0)
    full_ref[1] = dot3(normed, split(dk_ref[...]), 0, 0) + dot3(
        normed_out, split(odk_ref[...]), 0, 0
    )
    full_ref[2] = dot3(normed, split(dv_ref[...]), 0, 0) + dot3(
        normed_out, split(odv_ref[...]), 0, 0
    )
    for target, at in ((own_ref, mine), (send_ref, other)):
        target[:half, :half] = full_ref[0, at, :]
        target[:half, half:] = full_ref[1, at, :]
        target[half:, :half] = full_ref[2, at, :]
        target[half:, half:] = gmw_ref[at, part * half : (part + 1) * half]


def rows_grad_kernel(groups, crossing, scale, place_ref, unit_ref, halo_ref, far_ref, *refs):
    parts, refs = (refs[:5], refs[5:10]), refs[10:]
    qw_ref, kw_ref, vw_ref, mid_ref = refs[:4]
    gib_refs, refs = refs[4:6], refs[6:]
    vec_ref, gnorm_ref, inner_ref, outer_ref = refs[:4]
    gfar_refs = refs[4:]
    joined = lambda index: jnp.concatenate([part[index][...] for part in parts], axis=1)
    width = unit_ref.shape[-1]
    unit = unit_ref[...]
    outside = jnp.concatenate([halo_ref[...], far_ref[...]], axis=0)
    dq_f, dv_f, odv_f = joined(0) * scale, joined(2), joined(4)
    dq, dk, dv = split(dq_f), split(joined(1)), split(dv_f)
    odk, odv = split(joined(3)), split(odv_f)
    qw, kw, vw = split(qw_ref[...]), split(kw_ref[...]), split(vw_ref[...])
    gnorm = dot3(dq, qw, 1, 1) + dot3(dk, kw, 1, 1) + dot3(dv, vw, 1, 1)
    gout = dot3(odk, kw, 1, 1) + dot3(odv, vw, 1, 1)
    gnorm_ref[...] = gnorm
    odd = place_ref[ODD].astype(f32)
    far = far_ref.shape[0] // groups
    for group in range(groups):
        at = group * 2 * BLOCK
        low, high = gout[at : at + BLOCK], gout[at + BLOCK : at + 2 * BLOCK]
        inner_ref[group] = low * odd + high * (1.0 - odd)
        outer_ref[group] = low * (1.0 - odd) + high * odd
        for level, gfar_ref in enumerate(gfar_refs):
            at = groups * 2 * BLOCK + group * far + level * BLOCK
            gfar_ref[group] = gout[at : at + BLOCK]
    first = place_ref[CORE].astype(f32)
    other_gib, own_gib = gib_refs[0][...], gib_refs[1][...]
    low_gib = own_gib * (1.0 - first) + other_gib * first
    high_gib = own_gib * first + other_gib * (1.0 - first)
    vec_ref[...] = jnp.concatenate(
        [
            jnp.sum(gnorm * unit, axis=0, keepdims=True)
            + jnp.sum(gout * outside, axis=0, keepdims=True),
            jnp.sum(gnorm, axis=0, keepdims=True) + jnp.sum(gout, axis=0, keepdims=True),
            jnp.sum(dq_f, axis=0, keepdims=True),
            jnp.sum(dv_f, axis=0, keepdims=True) + jnp.sum(odv_f, axis=0, keepdims=True),
            mid_ref[0:4, :],
            low_gib[:, :width],
            low_gib[:, width:],
            high_gib[:, :width],
            high_gib[:, width:],
            jnp.zeros((SPARE - 12, width), f32),
        ],
        axis=0,
    )


def first_grad_kernel(
    groups, span, place_ref, gmid_ref, gnorm_ref, got_ref, mine_ref, outer_ref, unit_ref, inv_ref,
    gain_ref, out_ref, total_ref,
):
    width = gmid_ref.shape[-1]
    runs = span // BLOCK
    for group in range(groups):
        own = slice(group * span, (group + 1) * span)
        four = (got_ref[group, BLOCK:, :] + mine_ref[group]) * (1.0 / runs)
        spread = jnp.broadcast_to(four.reshape(BLOCK, 1, width), (BLOCK, runs, width)).reshape(
            span, width
        )
        total_ref[own, :] = gnorm_ref[own, :] + spread
        inner_at = pl.ds(pl.multiple_of(group * span + place_ref[INNER], BLOCK), BLOCK)
        outer_at = pl.ds(pl.multiple_of(group * span + place_ref[OUTER], BLOCK), BLOCK)
        total_ref[inner_at, :] = total_ref[inner_at, :] + got_ref[group, :BLOCK, :]
        total_ref[outer_at, :] = total_ref[outer_at, :] + outer_ref[group]
    out_ref[...] = gmid_ref[...] + norm_grad(
        total_ref[...], unit_ref[...], inv_ref[...], gain_ref[...]
    )


def pair_matrix(few, many):
    row_ids = lax.broadcasted_iota(jnp.int32, (few, many), 0)
    col_ids = lax.broadcasted_iota(jnp.int32, (few, many), 1)
    return jnp.where(col_ids // 2 == row_ids, 0.5, 0.0).astype(bf16)


def coarser_kernel(slot, place_ref, own_ref, got_ref, out_ref):
    half = BLOCK // 2
    bit = place_ref[slot]
    matrix = pair_matrix(half, BLOCK)
    for ref, at in ((own_ref, bit), (got_ref, 1 - bit)):
        start = ref.shape[1] - BLOCK
        at = pl.multiple_of(at * half, half)
        for group in range(ref.shape[0]):
            out_ref[group, pl.ds(at, half), :] = exact_dot2(
                matrix, split(ref[group, start:, :])
            )


def finer_kernel(slot, with_rim, passing, place_ref, *refs):
    wide_ref, refs = refs[-1], refs[:-1]
    if passing:
        refs[-1][...] = refs[0][...]
        refs = refs[1:-1]
    mine_ref, send_ref = refs[-2:]
    *sums, part_ref = refs[: -2 - with_rim]
    half = BLOCK // 2
    bit = place_ref[slot]
    offset = send_ref.shape[1] - BLOCK
    matrix = pair_matrix(half, BLOCK)
    for group in range(mine_ref.shape[0]):
        if with_rim:
            send_ref[group, :BLOCK, :] = refs[-3][group]
        wide = sums[0][group]
        for other in sums[1:]:
            wide = wide + other[group]
        wide_ref[...] = wide

        def handed(at):
            at = pl.ds(pl.multiple_of(at * half, half), half)
            return exact_dot2(matrix, split(wide_ref[at, :]), 0, 0)

        mine_ref[group] = handed(bit)
        send_ref[group, offset:, :] = handed(1 - bit) + part_ref[group]


def fold_kernel(slot, size, extra, place_ref, keep_ref, got_ref, *refs):
    if extra == "fresh":
        fresh_ref, refs = refs[0], refs[1:]
    if slot is None:
        refs[0][...] = keep_ref[:size, :] + got_ref[:size, :]
        if extra:
            refs[1][...] = keep_ref[size:, :] + got_ref[size:, :]
        return
    half = size // 2
    bit = place_ref[slot]
    for target, side in zip(refs, (bit, 1 - bit)):
        at = pl.ds(pl.multiple_of(side * half, half), half)
        target[:half, :] = keep_ref[at, :] + got_ref[at, :]
        if extra == "fresh":
            target[half:, :] = fresh_ref[...]
        elif extra:
            target[half:, :] = keep_ref[size:, :] + got_ref[size:, :]


def share_kernel(size, extra, place_ref, keep_ref, got_ref, *refs):
    keep, send = refs
    keep[...] = keep_ref[...] + got_ref[...]
    send[...] = keep[...]


def join_kernel(slot, place_ref, own_ref, got_ref, *refs):
    out_ref = refs[-1]
    half = own_ref.shape[0]
    bit = place_ref[slot]
    for source, side in ((own_ref, bit), (got_ref, 1 - bit)):
        out_ref[pl.ds(pl.multiple_of(side * half, half), half), :] = source[...]
    if len(refs) == 2:
        out_ref[2 * half :, :] = refs[0][...]


def run_copies(copies, sems):
    copies = [
        pltpu.make_async_copy(source, target, sems.at[index])
        for index, (source, target) in enumerate(copies)
    ]
    for copy in copies:
        copy.start()
    for copy in copies:
        copy.wait()


def place_outer_kernel(place_ref, own_ref, sib_ref, out_ref, sems):
    core, size = place_ref[CORE], own_ref.shape[0]
    run_copies(
        [
            (source, out_ref.at[pl.ds(pl.multiple_of(side * size, size), size), :])
            for source, side in ((own_ref, core), (sib_ref, 1 - core))
        ],
        sems,
    )


def place_inner_kernel(place_ref, own_ref, sib_ref, out_ref, sems):
    core, size = place_ref[CORE], out_ref.shape[0]
    copies = []
    for source, side in ((own_ref, core), (sib_ref, 1 - core)):
        for index in range(2):
            at = pl.ds(pl.multiple_of((side * 2 + index) * size, size), size)
            copies.append((source.at[index * size : (index + 1) * size, :], out_ref.at[:, at]))
    run_copies(copies, sems)


def place_square_kernel(part, place_ref, own_ref, sib_ref, *refs):
    *outs, sems = refs[-5:]
    half = outs[0].shape[0] // 2
    core = place_ref[CORE]
    copies = []
    for slot, out_ref in enumerate(outs):
        down, across = slot // 2 * half, slot % 2 * half
        for source, side in ((own_ref, core), (sib_ref, 1 - core)):
            at = pl.ds(pl.multiple_of(side * half, half), half)
            copies.append(
                (
                    source.at[down : down + half, across : across + half],
                    out_ref.at[at, part * half : (part + 1) * half],
                )
            )
    run_copies(copies, sems)


def vectors_kernel(own_ref, sib_ref, *outs):
    last = own_ref.shape[0] - SPARE
    vec_ref = own_ref[last:, :] + sib_ref[last:, :]
    for index, out in enumerate(outs):
        if index < 8:
            out[...] = vec_ref[index : index + 1, :]
        else:
            width = vec_ref.shape[-1]
            for part in range(4):
                out[:, part * width : (part + 1) * width] = vec_ref[8 + part : 9 + part, :]


def level_tables(span, crossing):
    half = span // 2
    top = int(math.log2(span // BLOCK // 2)) + crossing
    local_top = top - crossing
    expand = np.zeros((span, span), np.float32)
    means = np.zeros((span, span), np.float32)
    levels, at = [], 0
    for level in range(1, top + 1):
        count = span >> level
        for row in range(count):
            expand[at + row, row << level : (row + 1) << level] = 1.0
            means[at + row, row << level : (row + 1) << level] = 0.5**level
        levels.append((level, at, count))
        at += count
    near = np.full((half + 2 * BLOCK, half), FAR, np.float32)
    for query_block in range(half // BLOCK):
        near[
            query_block * BLOCK : (query_block + 3) * BLOCK,
            query_block * BLOCK : (query_block + 1) * BLOCK,
        ] = 0.0
    local_rows = sum(count for level, _, count in levels if level <= local_top)
    coarse = np.full((local_rows + BLOCK * crossing, span), FAR, np.float32)
    for level, start, count in levels:
        if level <= local_top:
            for block in range(count // BLOCK):
                key = start + (block ^ 1) * BLOCK
                query = start + block * BLOCK
                coarse[key : key + BLOCK, query : query + BLOCK] = level
        else:
            key = local_rows + (level - local_top - 1) * BLOCK
            coarse[key : key + BLOCK, start : start + count] = level
    one = coarse[:half, :half]
    rest = coarse[half:, half:]
    twice = lambda table: jnp.asarray(np.concatenate([table, table], axis=1))
    return (
        jnp.asarray(expand, bf16),
        jnp.asarray(means, bf16),
        twice(near),
        twice(one),
        twice(rest),
    )


class Here:
    def __init__(self, span, seq_count, steps):
        self.span, self.seq_count, self.steps = span, seq_count, steps

    def __getitem__(self, slot):
        seq, batch = lax.axis_index("seq"), lax.axis_index("batch")
        odd, core = seq & 1, batch & 1
        if slot == INNER:
            return (1 - odd) * (self.span - BLOCK)
        if slot == OUTER:
            return odd * (self.span - BLOCK)
        if slot == ODD:
            return odd
        if slot == FIRST:
            return (seq == 0).astype(jnp.int32)
        if slot == LAST:
            return (seq == self.seq_count - 1).astype(jnp.int32)
        if slot == CORE:
            return core
        slot -= CORE + 1
        crossing = self.seq_count.bit_length() - 1
        if slot < crossing:
            return seq >> slot & 1
        sides = [(batch, seq)[axis] >> bit & 1 for axis, bit in self.steps[slot - crossing]]
        return sides[0] + core * (sides[1] - sides[0])


class Order:
    def __init__(self):
        self.last = None

    def call(self, kernel, outs, ins, tag="", scratch=(), limit=8, spaces=None, out_space=VMEM,
             aliases=None):
        shapes = tuple(
            shape if isinstance(shape, jax.ShapeDtypeStruct) else jax.ShapeDtypeStruct(shape, f32)
            for shape in outs
        )
        spaces, aliases = spaces or {}, aliases or {}
        given = [index for index, value in enumerate(ins) if not isinstance(value, Here)]
        count, before = len(given), [] if self.last is None else [self.last]
        first_out = count + len(before)
        last_out = first_out + len(outs)

        def body(*refs):
            refs[last_out][...] = jnp.zeros(TOKEN, f32)
            taken = list(ins)
            for index, ref in zip(given, refs):
                taken[index] = ref
            kernel(*taken, *refs[first_out:last_out], *refs[last_out + 1 :])

        *results, self.last = pl.pallas_call(
            body,
            out_shape=shapes + (jax.ShapeDtypeStruct(TOKEN, f32),),
            in_specs=[spaces.get(index, VMEM) for index in given] + [ANY] * len(before),
            out_specs=tuple(out_space for _ in outs) + (VMEM,),
            name=getattr(kernel, "func", kernel).__name__ + str(tag),
            scratch_shapes=list(scratch),
            input_output_aliases={given.index(index): out for index, out in aliases.items()},
            cost_estimate=pl.CostEstimate(
                flops=COST, bytes_accessed=0, transcendentals=0
            ),
            compiler_params=pltpu.CompilerParams(vmem_limit_bytes=limit << 20),
        )(*[ins[index] for index in given], *before)
        return results


class Everywhere:
    def __init__(self, batch_count, seq_count):
        self.counts = batch_count, seq_count
        across = batch_count.bit_length() - 1
        along = seq_count.bit_length() - 1
        wide = [(0, bit) for bit in range(1, across)]
        tail = [(1, bit) for bit in range(1, along)]
        self.steps = list(zip(wide + [(1, 0)] + tail, [(1, 0)] + wide + tail))
        self.core = ((0, 0), (0, 0))

    def swap(self, array, step):
        batch_count, seq_count = self.counts
        pairs = []
        for batch in range(batch_count):
            for seq in range(seq_count):
                axis, bit = step[batch % 2]
                other = (batch ^ 1 << bit, seq) if axis == 0 else (batch, seq ^ 1 << bit)
                pairs.append((batch * seq_count + seq, other[0] * seq_count + other[1]))
        return lax.ppermute(array, ("batch", "seq"), pairs)

    def chunk(self, call, place, slot, kept, got, extra=None):
        size, width = kept.shape
        more = 0 if extra is None else extra.shape[0]
        keep = kept
        for index, step in enumerate(self.steps):
            fresh = extra is not None and index == 0
            mode = "fresh" if fresh else extra is not None
            keep, send = call(
                functools.partial(fold_kernel, slot + index, size, mode),
                [(size // 2 + more, width)] * 2,
                [place, keep, got] + ([extra] if fresh else []),
            )
            size //= 2
            got = self.swap(send, step)
            if index + 2 == len(self.steps):
                break
            yield
        yield
        keep, send = call(
            functools.partial(share_kernel, size, more),
            [(size + more, width)] * 2, [place, keep, got],
        )
        got = self.swap(send, self.steps[-1])
        yield
        own = call(
            functools.partial(fold_kernel, None, size, extra is not None),
            [(size, width)] + ([(more, width)] if more else []), [place, keep, got],
        )
        own, rest = own[0], own[1:]
        for index in range(len(self.steps) - 2, -1, -1):
            got = self.swap(own, self.steps[index])
            yield
            last = list(rest) if index == 0 else []
            (own,) = call(
                functools.partial(join_kernel, slot + index),
                [(2 * size + (more if last else 0), width)], [place, own, got] + last,
            )
            size *= 2
        return own, self.swap(own, self.core)


class Run:
    def __init__(self, turns):
        self.turns, self.result = turns, None

    def step(self, count=1):
        for _ in range(count if self.result is None else 0):
            try:
                next(self.turns)
            except StopIteration as end:
                self.result = end.value


def per_device(
    inputs, norm_gain, norm_bias, query_weight, query_bias, key_weight, value_weight, value_bias,
    mixer_weight, mixer_bias, final_gain, final_bias, inner_weight, inner_bias, outer_weight,
    outer_bias, cotangent,
):
    groups, span, width = inputs.shape
    tokens = groups * span
    half = span // 2
    hidden_width = inner_weight.shape[1]
    block = hidden_width // 4
    seq_count, batch_count = lax.axis_size("seq"), lax.axis_size("batch")
    crossing = seq_count.bit_length() - 1
    far_rows = BLOCK * crossing
    expand, means, near, one, rest = level_tables(span, crossing)
    coarse = means.shape[0]
    row = lambda vec: vec.reshape(1, -1)
    scale = 1.0 / math.sqrt(width // HEADS)
    x = inputs.reshape(tokens, width)
    cot = cotangent.reshape(tokens, width)
    everywhere = Everywhere(batch_count, seq_count)
    seq_slot = CORE + 1
    step_slot = seq_slot + crossing
    place = Here(span, seq_count, everywhere.steps)
    inner_pairs = [(i, i ^ 1) for i in range(seq_count)]
    outer_pairs = [
        (i, j)
        for i in range(seq_count)
        for j in [i + 1 if i % 2 else i - 1]
        if 0 <= j < seq_count
    ]
    order = Order()
    gain, shift = row(norm_gain), row(norm_bias)
    part_of_feed = hidden_width // 2
    narrow = lambda *shape: jax.ShapeDtypeStruct(shape, bf16)
    at = types.SimpleNamespace(hidden={}, gib={}, pairs={}, kept={}, got={}, fine={}, rough={})
    sums, turns = {}, {}

    call = order.call

    def start_sum(name, send, extra=None):
        at.got[name] = everywhere.swap(send, everywhere.core)

    def turn(name):
        if name not in sums:
            turns[name] = 0
            extra = at.vec if name == "D" else None
            sums[name] = Run(
                everywhere.chunk(
                    lambda *rest: call(*rest, name + str(turns[name])), place, step_slot, at.kept[name], at.got[name],
                    extra,
                )
            )
        sums[name].step()
        turns[name] += 1

    def first_norm():
        at.unit, at.inv, at.inner_send, outer_send = call(
            functools.partial(first_norm_kernel, groups, span),
            [(tokens, width), (tokens, 1), (groups, 2 * BLOCK, width), (groups, BLOCK, width)],
            [place, x],
        )
        at.far = [lax.ppermute(at.inner_send, "seq", inner_pairs)]
        at.outer_got = lax.ppermute(outer_send, "seq", outer_pairs)
        at.coarse_own = at.inner_send

    def project(kinds):
        weights = {"q": query_weight, "k": key_weight, "v": value_weight}
        biases = {"q": [row(query_bias)], "k": [], "v": [row(value_bias)]}
        scales = {"q": scale * LOG2E, "k": None, "v": 1.0}
        outs = call(
            functools.partial(project_kernel, groups, span, [scales[kind] for kind in kinds]),
            [(tokens, width), (groups * coarse, width)] * len(kinds),
            [at.unit, gain, shift, means] + [weights[kind] for kind in kinds]
            + [bias for kind in kinds for bias in biases[kind]], kinds,
        )
        for index, kind in enumerate(kinds):
            at.fine[kind], at.rough[kind] = outs[2 * index], outs[2 * index + 1]

    def project_qk():
        project("qk")

    def project_v():
        project("v")

    def coarser():
        bit = len(at.far)
        (at.coarse_own,) = call(
            functools.partial(coarser_kernel, seq_slot + bit - 1),
            [(groups, BLOCK, width)], [place, at.coarse_own, at.far[-1]],
        )
        at.far.append(
            lax.ppermute(at.coarse_own, "seq", [(i, i ^ 1 << bit) for i in range(seq_count)])
        )

    def rest_coarser():
        while len(at.far) < crossing:
            coarser()

    def local():
        at.num, at.den, at.numc, at.denc, at.halo, at.hk, at.hv = call(
            functools.partial(local_kernel, groups, span),
            [(groups * width, span), (groups * HEADS, span), (groups * width, half),
             (groups * HEADS, half)] + [(groups * 2 * BLOCK, width)] * 3,
            [place] + [at.fine[kind] for kind in "qkv"] + [at.rough[kind] for kind in "qkv"]
            + [at.far[0], at.outer_got, gain, shift, key_weight, value_weight,
               row(value_bias), near, one],
            scratch=[pltpu.VMEM((2,) + near.shape, f32)],
        )

    def remote():
        ins = at.far + [x, at.num, at.den, at.numc, at.denc]
        ins += [at.rough[kind] for kind in "qkv"]
        ins += [
            gain, shift, key_weight, value_weight, row(value_bias), rest, expand, mixer_weight,
            row(mixer_bias), row(final_gain), row(final_bias), row(outer_bias), cot,
        ]
        (
            at.far_rows, at.rk, at.rv, at.mixed, at.rden, at.unit2, at.inv2,
            at.acc, *at.split
        ) = call(
            functools.partial(remote_kernel, groups, span, crossing),
            [(groups * far_rows, width)] * 3 + [(groups * width, span), (groups * HEADS, span),
             (tokens, width), (tokens, 1), (tokens, width)] + [narrow(tokens, width)] * 4,
            ins, scratch=[pltpu.VMEM((tokens, width), f32)],
        )

    def outer(own):
        joint, *at.hidden[own] = call(
            functools.partial(outer_kernel, own),
            [(part_of_feed, width)] + [narrow(tokens, part_of_feed)] * 2 + [(tokens, part_of_feed)],
            [place] + at.split + [inner_weight, row(inner_bias)], own, limit=16,
        )
        if own:
            at.kept["A"] = joint
        else:
            start_sum("A", joint)

    def inner(own):
        joint, at.gib[own], at.acc, at.gacc = call(
            functools.partial(inner_kernel, own),
            [(2 * width, part_of_feed // 2), (1, part_of_feed), (tokens, width), (tokens, width)],
            [place] + at.split + at.hidden[own] + [inner_weight, outer_weight, at.acc]
            + ([at.gacc] if own else []),
            own, limit=16,
        )
        if own:
            at.kept["B"] = joint
        else:
            start_sum("B", joint)

    def middle_grad():
        (
            at.gmid, at.gmw, at.vec_mid, at.gnum, at.gnumt, at.gden, at.gnumct,
            at.gdenc,
        ) = call(
            functools.partial(middle_grad_kernel, groups, span),
            [(tokens, width), (width, width), (8, width), (tokens, width), (groups * width, span),
             (groups * HEADS, span), (groups * width, coarse), (groups * HEADS, coarse)],
            [cot, at.gacc, at.unit2, at.inv2, row(final_gain), at.mixed, at.rden,
             mixer_weight, expand],
        )

    outside_rows = groups * (2 * BLOCK + far_rows)

    def pairs(part):
        at.pairs[part] = call(
            functools.partial(pairs_grad_kernel, groups, part, span),
            [(tokens, half_width)] * 3 + [(outside_rows, half_width)] * 2,
            [place] + [at.fine[kind] for kind in "qkv"] + [at.rough[kind] for kind in "qkv"]
            + [at.hk, at.hv, at.rk, at.rv, at.gnum, at.gnumt, at.gden, at.gnumct, at.gdenc, near, one,
               rest, means], part,
            scratch=[
                pltpu.VMEM((2,) + near.shape, f32),
                pltpu.VMEM((span + 2 * BLOCK, half_width), f32),
                pltpu.VMEM((span + 2 * BLOCK, half_width), f32),
                pltpu.VMEM((half + rest.shape[0], half_width), f32),
                pltpu.VMEM((half + rest.shape[0], half_width), f32),
                pltpu.VMEM((half_width, span), f32),
                pltpu.VMEM((half_width, coarse), f32),
            ],
        )

    half_width = width // 2

    def square(part):
        name = "CD"[part]
        at.kept[name], send = call(
            functools.partial(square_grad_kernel, part, scale),
            [(width, width)] * 2,
            [place, at.unit, at.halo, at.far_rows, gain, shift, at.gmw]
            + list(at.pairs[part]), part,
            scratch=[pltpu.VMEM((3, width, half_width), f32)],
        )
        start_sum(name, send)

    def rows_grad():
        at.vec, at.gnorm, at.inner_back, outer_back, *gfar = call(
            functools.partial(rows_grad_kernel, groups, crossing, scale),
            [(SPARE, width), (tokens, width)] + [(groups, BLOCK, width)] * (2 + crossing),
            [place, at.unit, at.halo, at.far_rows] + list(at.pairs[0])
            + list(at.pairs[1]) + [query_weight, key_weight, value_weight, at.vec_mid,
                                     at.gib[0], at.gib[1]],
        )
        at.outer_back = lax.ppermute(outer_back, "seq", outer_pairs)
        at.gfar = gfar
        at.back = [
            lax.ppermute(gfar[-1], "seq", [(i, i ^ 1 << crossing - 1) for i in range(seq_count)])
        ]
        at.back_bit = crossing - 1

    def finer():
        at.back_bit -= 1
        bit = at.back_bit
        rim = [] if bit else [at.inner_back]
        passing = [at.outer_back] if bit == crossing - 2 else []
        mine, send, *passed = call(
            functools.partial(finer_kernel, seq_slot + bit, len(rim), bool(passing)),
            [(groups, BLOCK, width), (groups, BLOCK * (1 + len(rim)), width)]
            + [value.shape for value in passing],
            [place] + passing + at.back + [at.gfar[bit]] + rim,
            scratch=[pltpu.VMEM((BLOCK, width), f32)],
        )
        if passed:
            at.outer_back = passed[0]
        at.back = [
            lax.ppermute(send, "seq", [(i, i ^ 1 << bit) for i in range(seq_count)]), mine
        ]

    def first_grad():
        while at.back_bit:
            finer()
        (at.inputs_grad,) = call(
            functools.partial(first_grad_kernel, groups, span),
            [(tokens, width)],
            [place, at.gmid, at.gnorm] + at.back
            + [at.outer_back, at.unit, at.inv, gain],
            scratch=[pltpu.VMEM((tokens, width), f32)],
        )

    def write(name, kernel, shapes, count, before=()):
        while name not in sums or sums[name].result is None:
            turn(name)
        ins = [place] + list(sums[name].result) + list(before)
        return call(
            kernel, shapes, ins, name, scratch=[pltpu.SemaphoreType.DMA((count,))],
            out_space=HBM, spaces={3 + index: HBM for index in range(len(before))},
            aliases={3 + index: index for index in range(len(before))},
        )

    def write_outer():
        at.gow = write("A", place_outer_kernel, [(hidden_width, width)], 2)

    def write_inner():
        at.giw = write("B", place_inner_kernel, [(width, hidden_width)], 4)

    def write_square(part):
        at.squares = write(
            "CD"[part], functools.partial(place_square_kernel, part), [(width, width)] * 4, 8,
            getattr(at, "squares", ()),
        )
        if part:
            at.vecs = call(
                vectors_kernel, [(1, width)] * 8 + [(1, hidden_width)],
                list(sums["D"].result),
            )

    acts = (
        first_norm, project_qk, project_v, coarser, rest_coarser, local, remote, outer, inner,
        middle_grad, pairs, square, rows_grad, finer, first_grad, write_outer, write_inner,
        write_square,
    )
    acts = {act.__name__: act for act in acts}
    for name in PLAN:
        if name.isupper():
            turn(name)
        else:
            acts[name.rstrip("01")](*[int(digit) for digit in name if digit.isdigit()])
    gng, gnb, gqb, gvb, gfg, gfb, gmb, gob, gib = [vec.reshape(-1) for vec in at.vecs]
    gqw, gkw, gvw, gmw = at.squares
    return (
        at.acc.reshape(inputs.shape), at.inputs_grad.reshape(inputs.shape), gng, gnb, gqw,
        gqb, gkw, gvw, gvb, gmw, gmb, gfg, gfb, at.giw[0], gib, at.gow[0], gob,
    )


def solution(mesh):
    split_spec = P("batch", "seq", None)
    return jax.shard_map(
        per_device,
        mesh=mesh,
        in_specs=(split_spec,) + (P(),) * 15 + (split_spec,),
        out_specs=(split_spec, split_spec) + (P(),) * 15,
        check_vma=False,
    )
```

profile of v0, /device:TPU:0, one launch (start us, length us, event | category | flops | bytes accessed | tf_op | source)
XLA Modules:
  0.0 195.7 jit_solution(6277906242358716151)
XLA Ops:
  2.4 3.0 %collective-permute-start = (f32[2,32,512]{2,1,0:T(8,128)S(1)}, f32[2,32,512]{2,1,0:T(8,128)S(1)}, u32[]{:S(2)}, u32[]{:S(2)}) collective-permute-start(f32[2,32,512]{2,1,0:T(8,128)S(1)} %get-tuple-element.223.refs_0_), channel_id=1, source_target_pairs={{0,1},{1,0},{2,3},{3,2},{4,5},{5,4},{6,7},{7,6},{8,9},{9,8},{10,11... | collective-permute-start | bytes 393224 | tf_op jit(solution)/shard_map/ppermute | solution.py:1047
  5.5 2.6 %project_kernelqk.1 = (f32[512,512]{1,0:T(8,128)S(1)}, f32[512,512]{1,0:T(8,128)S(1)}, f32[512,512]{1,0:T(8,128)S(1)}, f32[512,512]{1,0:T(8,128)S(1)}, f32[8,128]{1,0:T(8,128)S(1)}) custom-call(f32[512,512]{1,0:T(8,128)S(1)} %get-tuple-element.224.refs_0_.refs_5_, f32[1,512]{1,0:T(1,128)S(1)} %bitcast.43, f32[1,512]{1,0:T(1,128)S(1)} %bitcast.37, ...), custom_call_target="tpu_custom_call" | custom-call | flops 10000000000 | tf_op jit(solution)/shard_map/project_kernelqk/pallas_call | solution.py:897
  14.0 2.6 %collective-permute-start.2 = (f32[2,16,512]{2,1,0:T(8,128)S(1)}, f32[2,16,512]{2,1,0:T(8,128)S(1)}, u32[]{:S(2)}, u32[]{:S(2)}) collective-permute-start(f32[2,16,512]{2,1,0:T(8,128)S(1)} %get-tuple-element.230), channel_id=1, source_target_pairs={{0,4},{1,5},{2,6},{3,7},{4,0},{5,1},{6,2},{7,3},{8,12},{9,13},{10,... | collective-permute-start | bytes 196616 | tf_op jit(solution)/shard_map/ppermute | solution.py:1077
  16.8 4.1 %local_kernel.1 = (f32[1024,256]{1,0:T(8,128)S(1)}, f32[16,256]{1,0:T(8,128)S(1)}, f32[1024,128]{1,0:T(8,128)S(1)}, f32[16,128]{1,0:T(8,128)S(1)}, f32[64,512]{1...) custom-call(f32[512,512]{1,0:T(8,128)S(1)} %get-tuple-element.231.refs_0_, ...), custom_call_target="tpu_custom_call" | custom-call | flops 10000000000 | tf_op jit(solution)/shard_map/local_kernel/pallas_call | solution.py:897
  21.0 4.1 %remote_kernel.1 = (f32[96,512]{1,0:T(8,128)S(1)}, f32[96,512]{1,0:T(8,128)S(1)}, f32[96,512]{1,0:T(8,128)S(1)}, f32[1024,256]{1,0:T(8,128)S(1)}, f32[16,256]{1,...) custom-call(f32[2,32,512]{2,1,0:T(8,128)S(1)} %collective-permute-do, ...), custom_call_target="tpu_custom_call" | custom-call | flops 10000000000 | tf_op jit(solution)/shard_map/remote_kernel/pallas_call | solution.py:897
  25.2 4.0 %outer_kernel0.1 = (f32[1024,512]{1,0:T(8,128)S(1)}, bf16[512,1024]{1,0:T(8,128)(2,1)S(1)}, bf16[512,1024]{1,0:T(8,128)(2,1)S(1)}, f32[512,1024]{1,0:T(8,128)S(1)}, f32[8,128]{1,0:T(8,128)S(1)}) custom-call(bf16[512,512]{1,0:T(8,128)(2,1)S(1)} %get-tuple-element.244.refs_0_, bf16[512,512]{1,0:T(8,128)(2,1)S(1)} %get-tuple-element.245.refs_1_, ...), custom_call_target="tpu_custom_call" | custom-call | flops 10000000000 | tf_op jit(solution)/shard_map/outer_kernel0/pallas_call | solution.py:897
  29.2 4.1 %outer_kernel1.1 = (f32[1024,512]{1,0:T(8,128)S(1)}, bf16[512,1024]{1,0:T(8,128)(2,1)S(1)}, bf16[512,1024]{1,0:T(8,128)(2,1)S(1)}, f32[512,1024]{1,0:T(8,128)S(1)}, f32[8,128]{1,0:T(8,128)S(1)}) custom-call(bf16[512,512]{1,0:T(8,128)(2,1)S(1)} %get-tuple-element.244.refs_0_, bf16[512,512]{1,0:T(8,128)(2,1)S(1)} %get-tuple-element.245.refs_1_, ...), custom_call_target="tpu_custom_call" | custom-call | flops 10000000000 | tf_op jit(solution)/shard_map/outer_kernel1/pallas_call | solution.py:897
  33.4 6.8 %inner_kernel0.1 = (f32[1024,512]{1,0:T(8,128)S(1)}, f32[1,1024]{1,0:T(1,128)S(1)}, f32[512,512]{1,0:T(8,128)S(1)}, f32[512,512]{1,0:T(8,128)S(1)}, f32[8,128]{1,0:T(8,128)S(1)}) custom-call(bf16[512,512]{1,0:T(8,128)(2,1)S(1)} %get-tuple-element.244.refs_0_, bf16[512,512]{1,0:T(8,128)(2,1)S(1)} %get-tuple-element.245.refs_1_, ...), custom_call_target="tpu_custom_call" | custom-call | flops 10000000000 | tf_op jit(solution)/shard_map/inner_kernel0/pallas_call | solution.py:897
  42.6 6.8 %inner_kernel1.1 = (f32[1024,512]{1,0:T(8,128)S(1)}, f32[1,1024]{1,0:T(1,128)S(1)}, f32[512,512]{1,0:T(8,128)}, f32[512,512]{1,0:T(8,128)S(1)}, f32[8,128]{1,0:T(8,128)S(1)}) custom-call(bf16[512,512]{1,0:T(8,128)(2,1)S(1)} %get-tuple-element.244.refs_0_, bf16[512,512]{1,0:T(8,128)(2,1)S(1)} %get-tuple-element.245.refs_1_, ...), custom_call_target="tpu_custom_call" | custom-call | flops 10000000000 | tf_op jit(solution)/shard_map/inner_kernel1/pallas_call | solution.py:897
  49.3 3.1 %middle_grad_kernel.1 = (f32[512,512]{1,0:T(8,128)S(1)}, f32[512,512]{1,0:T(8,128)S(1)}, f32[8,512]{1,0:T(8,128)S(1)}, f32[512,512]{1,0:T(8,128)S(1)}, f32[1024,...) custom-call(f32[512,512]{1,0:T(8,128)S(1)} %bitcast.25, ...), custom_call_target="tpu_custom_call" | custom-call | flops 10000000000 | tf_op jit(solution)/shard_map/middle_grad_kernel/pallas_call | solution.py:897
  53.2 2.6 %collective-permute-done.5.refs_1_ = f32[512,512]{1,0:T(8,128)S(1)} collective-permute-done((f32[512,512]{1,0:T(8,128)S(1)}, f32[512,512]{1,0:T(8,128)S(1)}, u32[]{:S(2)}, u32[]{:S(2)}) %collective-permute-start.5) | collective-permute-done | bytes 1048608 | tf_op jit(solution)/shard_map/ppermute | solution.py:931
  56.0 3.0 %collective-permute-start.7 = (f32[256,512]{1,0:T(8,128)S(1)}, f32[256,512]{1,0:T(8,128)S(1)}, u32[]{:S(2)}, u32[]{:S(2)}) collective-permute-start(f32[256,512]{1,0:T(8,128)S(1)} %get-tuple-element.305), channel_id=1, source_target_pairs={{0,1},{1,0},{2,3},{3,2},{4,5},{5,4},{6,7},{7,6},{8,24},{9,25},{10,... | collective-permute-start | bytes 1572872 | tf_op jit(solution)/shard_map/ppermute | solution.py:931
  59.0 5.7 %pairs_grad_kernel0.1 = (f32[512,256]{1,0:T(8,128)S(1)}, f32[512,256]{1,0:T(8,128)S(1)}, f32[512,256]{1,0:T(8,128)S(1)}, f32[160,256]{1,0:T(8,128)S(1)}, f32[160,256]{1,0:T(8,128)S(1)}, /*index=5*/f32[8,128]{1,0:T(8,128)S(1)}) custom-call(f32[512,512]{1,0:T(8,128)S(1)} %get-tuple-element.231.refs_0_, f32[512,512]{1,0:T(8,128)S(1)} %get-tuple-element.232.refs_1_, ...), custom_call_target="tpu_custom_call" | custom-call | flops 10000000000 | tf_op jit(solution)/shard_map/pairs_grad_kernel0/pallas_call | solution.py:897
  64.7 5.9 %pairs_grad_kernel1.1 = (f32[512,256]{1,0:T(8,128)S(1)}, f32[512,256]{1,0:T(8,128)S(1)}, f32[512,256]{1,0:T(8,128)S(1)}, f32[160,256]{1,0:T(8,128)S(1)}, f32[160,256]{1,0:T(8,128)S(1)}, /*index=5*/f32[8,128]{1,0:T(8,128)S(1)}) custom-call(f32[512,512]{1,0:T(8,128)S(1)} %get-tuple-element.231.refs_0_, f32[512,512]{1,0:T(8,128)S(1)} %get-tuple-element.232.refs_1_, ...), custom_call_target="tpu_custom_call" | custom-call | flops 10000000000 | tf_op jit(solution)/shard_map/pairs_grad_kernel1/pallas_call | solution.py:897
  73.6 3.7 %rows_grad_kernel.1 = (f32[16,512]{1,0:T(8,128)S(1)}, f32[512,512]{1,0:T(8,128)S(1)}, f32[2,16,512]{2,1,0:T(8,128)S(1)}, f32[2,16,512]{2,1,0:T(8,128)S(1)}, f32[...) custom-call(f32[512,512]{1,0:T(8,128)S(1)} %copy-done.27, ...), custom_call_target="tpu_custom_call" | custom-call | flops 10000000000 | tf_op jit(solution)/shard_map/rows_grad_kernel/pallas_call | solution.py:897
  78.0 5.4 %collective-permute-start.9 = (f32[2,16,512]{2,1,0:T(8,128)S(1)}, f32[2,16,512]{2,1,0:T(8,128)S(1)}, u32[]{:S(2)}, u32[]{:S(2)}) collective-permute-start(f32[2,16,512]{2,1,0:T(8,128)S(1)} %get-tuple-element.310), channel_id=1, source_target_pairs={{0,4},{1,5},{2,6},{3,7},{4,0},{5,1},{6,2},{7,3},{8,12},{9,13},{10,... | collective-permute-start | bytes 196616 | tf_op jit(solution)/shard_map/ppermute | solution.py:1192
  83.5 2.1 %collective-permute-start.15 = (f32[256,512]{1,0:T(8,128)S(1)}, f32[256,512]{1,0:T(8,128)S(1)}, u32[]{:S(2)}, u32[]{:S(2)}) collective-permute-start(f32[256,512]{1,0:T(8,128)S(1)} %get-tuple-element.333), channel_id=1, source_target_pairs={{0,1},{1,0},{2,3},{3,2},{4,5},{5,4},{6,7},{7,6},{8,24},{9,25},{10,... | collective-permute-start | bytes 1572872 | tf_op jit(solution)/shard_map/ppermute | solution.py:931
  88.3 2.6 %collective-permute-start.17 = (f32[128,512]{1,0:T(8,128)S(1)}, f32[128,512]{1,0:T(8,128)S(1)}, u32[]{:S(2)}, u32[]{:S(2)}) collective-permute-start(f32[128,512]{1,0:T(8,128)S(1)} %get-tuple-element.339), channel_id=1, source_target_pairs={{0,4},{1,5},{2,6},{3,7},{4,0},{5,1},{6,2},{7,3},{8,12},{9,13},{10,... | collective-permute-start | bytes 786440 | tf_op jit(solution)/shard_map/ppermute | solution.py:931
  91.0 2.1 %square_grad_kernel0.1 = (f32[512,512]{1,0:T(8,128)S(1)}, f32[512,512]{1,0:T(8,128)S(1)}, f32[8,128]{1,0:T(8,128)S(1)}) custom-call(f32[512,512]{1,0:T(8,128)S(1)} %copy-done.27, f32[64,512]{1,0:T(8,128)S(1)} %get-tuple-element.272.refs_1_, f32[96,512]{1,0:T(8,128)S(1)} %get-tuple-element.273.refs_2_, f32[1,512]{1,0:T(1,128)S(1)} %bitcast.47, ...), custom_call_target="tpu_custom_call" | custom-call | flops 10000000000 | tf_op jit(solution)/shard_map/square_grad_kernel0/pallas_call | solution.py:897
  96.0 2.1 %square_grad_kernel1.1 = (f32[512,512]{1,0:T(8,128)S(1)}, f32[512,512]{1,0:T(8,128)S(1)}, f32[8,128]{1,0:T(8,128)S(1)}) custom-call(f32[512,512]{1,0:T(8,128)S(1)} %copy-done.27, f32[64,512]{1,0:T(8,128)S(1)} %get-tuple-element.272.refs_1_, f32[96,512]{1,0:T(8,128)S(1)} %get-tuple-element.273.refs_2_, f32[1,512]{1,0:T(1,128)S(1)} %bitcast.48, ...), custom_call_target="tpu_custom_call" | custom-call | flops 10000000000 | tf_op jit(solution)/shard_map/square_grad_kernel1/pallas_call | solution.py:897
  100.6 6.8 %collective-permute-done.16.refs_1_ = f32[256,512]{1,0:T(8,128)S(1)} collective-permute-done((f32[256,512]{1,0:T(8,128)S(1)}, f32[256,512]{1,0:T(8,128)S(1)}, u32[]{:S(2)}, u32[]{:S(2)}) %collective-permute-start.16) | collective-permute-done | bytes 524320 | tf_op jit(solution)/shard_map/ppermute | solution.py:931
  108.0 3.5 %collective-permute-done.20.refs_1_ = f32[128,512]{1,0:T(8,128)S(1)} collective-permute-done((f32[128,512]{1,0:T(8,128)S(1)}, f32[128,512]{1,0:T(8,128)S(1)}, u32[]{:S(2)}, u32[]{:S(2)}) %collective-permute-start.20) | collective-permute-done | bytes 262176 | tf_op jit(solution)/shard_map/ppermute | solution.py:931
  118.8 4.6 %collective-permute-done.25.refs_1_ = f32[256,512]{1,0:T(8,128)S(1)} collective-permute-done((f32[256,512]{1,0:T(8,128)S(1)}, f32[256,512]{1,0:T(8,128)S(1)}, u32[]{:S(2)}, u32[]{:S(2)}) %collective-permute-start.25) | collective-permute-done | bytes 524320 | tf_op jit(solution)/shard_map/ppermute | solution.py:931
  128.1 2.6 %collective-permute-start.29 = (f32[64,512]{1,0:T(8,128)S(1)}, f32[64,512]{1,0:T(8,128)S(1)}, u32[]{:S(2)}, u32[]{:S(2)}) collective-permute-start(f32[64,512]{1,0:T(8,128)S(1)} %get-tuple-element.375), channel_id=1, source_target_pairs={{0,4},{1,5},{2,6},{3,7},{4,0},{5,1},{6,2},{7,3},{8,12},{9,13},{10,... | collective-permute-start | bytes 393224 | tf_op jit(solution)/shard_map/ppermute | solution.py:931
  133.8 3.7 %collective-permute-done.29.refs_1_ = f32[64,512]{1,0:T(8,128)S(1)} collective-permute-done((f32[64,512]{1,0:T(8,128)S(1)}, f32[64,512]{1,0:T(8,128)S(1)}, u32[]{:S(2)}, u32[]{:S(2)}) %collective-permute-start.29) | collective-permute-done | bytes 131104 | tf_op jit(solution)/shard_map/ppermute | solution.py:931
  141.7 5.2 %collective-permute-done.27.refs_1_ = f32[80,512]{1,0:T(8,128)S(1)} collective-permute-done((f32[80,512]{1,0:T(8,128)S(1)}, f32[80,512]{1,0:T(8,128)S(1)}, u32[]{:S(2)}, u32[]{:S(2)}) %collective-permute-start.27) | collective-permute-done | bytes 163872 | tf_op jit(solution)/shard_map/ppermute | solution.py:931
  149.5 7.3 %collective-permute-done.30.refs_1_ = f32[80,512]{1,0:T(8,128)S(1)} collective-permute-done((f32[80,512]{1,0:T(8,128)S(1)}, f32[80,512]{1,0:T(8,128)S(1)}, u32[]{:S(2)}, u32[]{:S(2)}) %collective-permute-start.30) | collective-permute-done | bytes 163872 | tf_op jit(solution)/shard_map/ppermute | solution.py:931
  157.0 4.8 %collective-permute-done.33.refs_1_ = f32[64,512]{1,0:T(8,128)S(1)} collective-permute-done((f32[64,512]{1,0:T(8,128)S(1)}, f32[64,512]{1,0:T(8,128)S(1)}, u32[]{:S(2)}, u32[]{:S(2)}) %collective-permute-start.33) | collective-permute-done | bytes 131104 | tf_op jit(solution)/shard_map/ppermute | solution.py:931
  161.9 9.9 %collective-permute-done.36.refs_1_ = f32[512,512]{1,0:T(8,128)S(1)} collective-permute-done((f32[512,512]{1,0:T(8,128)S(1)}, f32[512,512]{1,0:T(8,128)S(1)}, u32[]{:S(2)}, u32[]{:S(2)}) %collective-permute-start.36) | collective-permute-done | bytes 1048608 | tf_op jit(solution)/shard_map/ppermute | solution.py:931
  172.1 2.3 %collective-permute-start.35 = (f32[128,512]{1,0:T(8,128)S(1)}, f32[128,512]{1,0:T(8,128)S(1)}, u32[]{:S(2)}, u32[]{:S(2)}) collective-permute-start(f32[128,512]{1,0:T(8,128)S(1)} %get-tuple-element.390.refs_0_), channel_id=1, source_target_pairs={{0,1},{1,0},{2,3},{3,2},{4,5},{5,4},{6,7},{7,6},{8,24},{9,25},{10,... | collective-permute-start | bytes 786440 | tf_op jit(solution)/shard_map/ppermute | solution.py:931
  175.0 6.1 %collective-permute-done.35.refs_1_ = f32[128,512]{1,0:T(8,128)S(1)} collective-permute-done((f32[128,512]{1,0:T(8,128)S(1)}, f32[128,512]{1,0:T(8,128)S(1)}, u32[]{:S(2)}, u32[]{:S(2)}) %collective-permute-start.35) | collective-permute-done | bytes 262176 | tf_op jit(solution)/shard_map/ppermute | solution.py:931
  185.9 4.5 %collective-permute-done.38.refs_1_ = f32[256,512]{1,0:T(8,128)S(1)} collective-permute-done((f32[256,512]{1,0:T(8,128)S(1)}, f32[256,512]{1,0:T(8,128)S(1)}, u32[]{:S(2)}, u32[]{:S(2)}) %collective-permute-start.38) | collective-permute-done | bytes 524320 | tf_op jit(solution)/shard_map/ppermute | solution.py:931
  (169 shorter events, 56.1 us)
Async XLA Ops:
  29.1 11.6 %collective-permute-start.4 = (f32[1024,512]{1,0:T(8,128)S(1)}, f32[1024,512]{1,0:T(8,128)S(1)}, u32[]{:S(2)}, u32[]{:S(2)}) collective-permute-start(f32[1024,512]{1,0:T(8,128)S(1)} %get-tuple-element.261), channel_id=1, source_target_pairs={{0,8},{1,9},{2,10},{3,11},{4,12},{5,13},{6,14},{7,15},{8,0},{9,1},... | collective-permute-start | bytes 6291464 | tf_op jit(solution)/shard_map/ppermute | solution.py:931
  40.2 12.2 %collective-permute-start.6 = (f32[1024,512]{1,0:T(8,128)S(1)}, f32[1024,512]{1,0:T(8,128)S(1)}, u32[]{:S(2)}, u32[]{:S(2)}) collective-permute-start(f32[1024,512]{1,0:T(8,128)S(1)} %get-tuple-element.286), channel_id=1, source_target_pairs={{0,8},{1,9},{2,10},{3,11},{4,12},{5,13},{6,14},{7,15},{8,0},{9,1},... | collective-permute-start | bytes 6291464 | tf_op jit(solution)/shard_map/ppermute | solution.py:931
  41.0 14.9 %collective-permute-start.5 = (f32[512,512]{1,0:T(8,128)S(1)}, f32[512,512]{1,0:T(8,128)S(1)}, u32[]{:S(2)}, u32[]{:S(2)}) collective-permute-start(f32[512,512]{1,0:T(8,128)S(1)} %get-tuple-element.284), channel_id=1, source_target_pairs={{0,16},{1,17},{2,18},{3,19},{4,20},{5,21},{6,22},{7,23},{8,9},{9,8... | collective-permute-start | bytes 3145736 | tf_op jit(solution)/shard_map/ppermute | solution.py:931
  52.6 30.7 %collective-permute-start.11 = (f32[512,512]{1,0:T(8,128)S(1)}, f32[512,512]{1,0:T(8,128)S(1)}, u32[]{:S(2)}, u32[]{:S(2)}) collective-permute-start(f32[512,512]{1,0:T(8,128)S(1)} %get-tuple-element.315), channel_id=1, source_target_pairs={{0,16},{1,17},{2,18},{3,19},{4,20},{5,21},{6,22},{7,23},{8,9},{9,8... | collective-permute-start | bytes 3145736 | tf_op jit(solution)/shard_map/ppermute | solution.py:931
  56.0 15.8 %collective-permute-start.7 = (f32[256,512]{1,0:T(8,128)S(1)}, f32[256,512]{1,0:T(8,128)S(1)}, u32[]{:S(2)}, u32[]{:S(2)}) collective-permute-start(f32[256,512]{1,0:T(8,128)S(1)} %get-tuple-element.305), channel_id=1, source_target_pairs={{0,1},{1,0},{2,3},{3,2},{4,5},{5,4},{6,7},{7,6},{8,24},{9,25},{10,... | collective-permute-start | bytes 1572872 | tf_op jit(solution)/shard_map/ppermute | solution.py:931
  71.9 13.7 %collective-permute-start.10 = (f32[128,512]{1,0:T(8,128)S(1)}, f32[128,512]{1,0:T(8,128)S(1)}, u32[]{:S(2)}, u32[]{:S(2)}) collective-permute-start(f32[128,512]{1,0:T(8,128)S(1)} %get-tuple-element.313), channel_id=1, source_target_pairs={{0,2},{1,3},{2,0},{3,1},{4,6},{5,7},{6,4},{7,5},{8,10},{9,11},{10,... | collective-permute-start | bytes 786440 | tf_op jit(solution)/shard_map/ppermute | solution.py:931
  77.3 8.4 %collective-permute-start.8 = (f32[2,16,512]{2,1,0:T(8,128)S(1)}, f32[2,16,512]{2,1,0:T(8,128)S(1)}, u32[]{:S(2)}, u32[]{:S(2)}) collective-permute-start(f32[2,16,512]{2,1,0:T(8,128)S(1)} %get-tuple-element.309), channel_id=1, source_target_pairs={{1,2},{2,1},{3,4},{4,3},{5,6},{6,5},{9,10},{10,9},{11,12},{12,11},... | collective-permute-start | bytes 196616 | tf_op jit(solution)/shard_map/ppermute | solution.py:1189
  83.5 10.4 %collective-permute-start.15 = (f32[256,512]{1,0:T(8,128)S(1)}, f32[256,512]{1,0:T(8,128)S(1)}, u32[]{:S(2)}, u32[]{:S(2)}) collective-permute-start(f32[256,512]{1,0:T(8,128)S(1)} %get-tuple-element.333), channel_id=1, source_target_pairs={{0,1},{1,0},{2,3},{3,2},{4,5},{5,4},{6,7},{7,6},{8,24},{9,25},{10,... | collective-permute-start | bytes 1572872 | tf_op jit(solution)/shard_map/ppermute | solution.py:931
  88.3 12.0 %collective-permute-start.17 = (f32[128,512]{1,0:T(8,128)S(1)}, f32[128,512]{1,0:T(8,128)S(1)}, u32[]{:S(2)}, u32[]{:S(2)}) collective-permute-start(f32[128,512]{1,0:T(8,128)S(1)} %get-tuple-element.339), channel_id=1, source_target_pairs={{0,4},{1,5},{2,6},{3,7},{4,0},{5,1},{6,2},{7,3},{8,12},{9,13},{10,... | collective-permute-start | bytes 786440 | tf_op jit(solution)/shard_map/ppermute | solution.py:931
  93.4 22.0 %collective-permute-start.13 = (f32[2,32,512]{2,1,0:T(8,128)S(1)}, f32[2,32,512]{2,1,0:T(8,128)S(1)}, u32[]{:S(2)}, u32[]{:S(2)}) collective-permute-start(f32[2,32,512]{2,1,0:T(8,128)S(1)} %get-tuple-element.326), channel_id=1, source_target_pairs={{0,1},{1,0},{2,3},{3,2},{4,5},{5,4},{6,7},{7,6},{8,9},{9,8},{10,11... | collective-permute-start | bytes 393224 | tf_op jit(solution)/shard_map/ppermute | solution.py:1211
  94.0 17.5 %collective-permute-start.19 = (f32[128,512]{1,0:T(8,128)S(1)}, f32[128,512]{1,0:T(8,128)S(1)}, u32[]{:S(2)}, u32[]{:S(2)}) collective-permute-start(f32[128,512]{1,0:T(8,128)S(1)} %get-tuple-element.346), channel_id=1, source_target_pairs={{0,2},{1,3},{2,0},{3,1},{4,6},{5,7},{6,4},{7,5},{8,10},{9,11},{10,... | collective-permute-start | bytes 786440 | tf_op jit(solution)/shard_map/ppermute | solution.py:931
  98.1 9.2 %collective-permute-start.16 = (f32[256,512]{1,0:T(8,128)S(1)}, f32[256,512]{1,0:T(8,128)S(1)}, u32[]{:S(2)}, u32[]{:S(2)}) collective-permute-start(f32[256,512]{1,0:T(8,128)S(1)} %get-tuple-element.337), channel_id=1, source_target_pairs={{0,16},{1,17},{2,18},{3,19},{4,20},{5,21},{6,22},{7,23},{8,9},{9,8... | collective-permute-start | bytes 1572872 | tf_op jit(solution)/shard_map/ppermute | solution.py:931
  100.4 11.1 %collective-permute-start.20 = (f32[128,512]{1,0:T(8,128)S(1)}, f32[128,512]{1,0:T(8,128)S(1)}, u32[]{:S(2)}, u32[]{:S(2)}) collective-permute-start(f32[128,512]{1,0:T(8,128)S(1)} %get-tuple-element.347.refs_0_), channel_id=1, source_target_pairs={{0,2},{1,3},{2,0},{3,1},{4,6},{5,7},{6,4},{7,5},{8,10},{9,11},{10,... | collective-permute-start | bytes 786440 | tf_op jit(solution)/shard_map/ppermute | solution.py:931
  100.5 16.5 %collective-permute-start.21 = (f32[512,512]{1,0:T(8,128)S(1)}, f32[512,512]{1,0:T(8,128)S(1)}, u32[]{:S(2)}, u32[]{:S(2)}) collective-permute-start(f32[512,512]{1,0:T(8,128)S(1)} %get-tuple-element.354), channel_id=1, source_target_pairs={{0,8},{1,9},{2,10},{3,11},{4,12},{5,13},{6,14},{7,15},{8,0},{9,1},... | collective-permute-start | bytes 3145736 | tf_op jit(solution)/shard_map/ppermute | solution.py:931
  111.6 13.8 %collective-permute-start.23 = (f32[128,512]{1,0:T(8,128)S(1)}, f32[128,512]{1,0:T(8,128)S(1)}, u32[]{:S(2)}, u32[]{:S(2)}) collective-permute-start(f32[128,512]{1,0:T(8,128)S(1)} %get-tuple-element.360), channel_id=1, source_target_pairs={{0,4},{1,5},{2,6},{3,7},{4,0},{5,1},{6,2},{7,3},{8,12},{9,13},{10,... | collective-permute-start | bytes 786440 | tf_op jit(solution)/shard_map/ppermute | solution.py:931
  111.7 11.6 %collective-permute-start.25 = (f32[256,512]{1,0:T(8,128)S(1)}, f32[256,512]{1,0:T(8,128)S(1)}, u32[]{:S(2)}, u32[]{:S(2)}) collective-permute-start(f32[256,512]{1,0:T(8,128)S(1)} %get-tuple-element.363.refs_0_), channel_id=1, source_target_pairs={{0,1},{1,0},{2,3},{3,2},{4,5},{5,4},{6,7},{7,6},{8,24},{9,25},{10,... | collective-permute-start | bytes 1572872 | tf_op jit(solution)/shard_map/ppermute | solution.py:931
  113.9 9.5 %collective-permute-start.24 = (f32[64,512]{1,0:T(8,128)S(1)}, f32[64,512]{1,0:T(8,128)S(1)}, u32[]{:S(2)}, u32[]{:S(2)}) collective-permute-start(f32[64,512]{1,0:T(8,128)S(1)} %get-tuple-element.362), channel_id=1, source_target_pairs={{0,2},{1,3},{2,0},{3,1},{4,6},{5,7},{6,4},{7,5},{8,10},{9,11},{10,... | collective-permute-start | bytes 393224 | tf_op jit(solution)/shard_map/ppermute | solution.py:931
  117.2 9.6 %collective-permute-start.22 = (f32[272,512]{1,0:T(8,128)S(1)}, f32[272,512]{1,0:T(8,128)S(1)}, u32[]{:S(2)}, u32[]{:S(2)}) collective-permute-start(f32[272,512]{1,0:T(8,128)S(1)} %get-tuple-element.358), channel_id=1, source_target_pairs={{0,16},{1,17},{2,18},{3,19},{4,20},{5,21},{6,22},{7,23},{8,9},{9,8... | collective-permute-start | bytes 1671176 | tf_op jit(solution)/shard_map/ppermute | solution.py:931
  128.1 9.4 %collective-permute-start.29 = (f32[64,512]{1,0:T(8,128)S(1)}, f32[64,512]{1,0:T(8,128)S(1)}, u32[]{:S(2)}, u32[]{:S(2)}) collective-permute-start(f32[64,512]{1,0:T(8,128)S(1)} %get-tuple-element.375), channel_id=1, source_target_pairs={{0,4},{1,5},{2,6},{3,7},{4,0},{5,1},{6,2},{7,3},{8,12},{9,13},{10,... | collective-permute-start | bytes 393224 | tf_op jit(solution)/shard_map/ppermute | solution.py:931
  130.6 11.0 %collective-permute-start.28 = (f32[128,512]{1,0:T(8,128)S(1)}, f32[128,512]{1,0:T(8,128)S(1)}, u32[]{:S(2)}, u32[]{:S(2)}) collective-permute-start(f32[128,512]{1,0:T(8,128)S(1)} %get-tuple-element.373.refs_0_), channel_id=1, source_target_pairs={{0,2},{1,3},{2,0},{3,1},{4,6},{5,7},{6,4},{7,5},{8,10},{9,11},{10,... | collective-permute-start | bytes 786440 | tf_op jit(solution)/shard_map/ppermute | solution.py:931
  130.6 18.0 %collective-permute-start.32 = (f32[512,512]{1,0:T(8,128)S(1)}, f32[512,512]{1,0:T(8,128)S(1)}, u32[]{:S(2)}, u32[]{:S(2)}) collective-permute-start(f32[512,512]{1,0:T(8,128)S(1)} %get-tuple-element.382.refs_0_), channel_id=1, source_target_pairs={{0,16},{1,17},{2,18},{3,19},{4,20},{5,21},{6,22},{7,23},{8,9},{9,8... | collective-permute-start | bytes 3145736 | tf_op jit(solution)/shard_map/ppermute | solution.py:931
  137.5 11.3 %collective-permute-start.31 = (f32[64,512]{1,0:T(8,128)S(1)}, f32[64,512]{1,0:T(8,128)S(1)}, u32[]{:S(2)}, u32[]{:S(2)}) collective-permute-start(f32[64,512]{1,0:T(8,128)S(1)} %get-tuple-element.381.refs_0_), channel_id=1, source_target_pairs={{0,2},{1,3},{2,0},{3,1},{4,6},{5,7},{6,4},{7,5},{8,10},{9,11},{10,... | collective-permute-start | bytes 393224 | tf_op jit(solution)/shard_map/ppermute | solution.py:931
  137.6 9.4 %collective-permute-start.27 = (f32[80,512]{1,0:T(8,128)S(1)}, f32[80,512]{1,0:T(8,128)S(1)}, u32[]{:S(2)}, u32[]{:S(2)}) collective-permute-start(f32[80,512]{1,0:T(8,128)S(1)} %get-tuple-element.372), channel_id=1, source_target_pairs={{0,2},{1,3},{2,0},{3,1},{4,6},{5,7},{6,4},{7,5},{8,10},{9,11},{10,... | collective-permute-start | bytes 491528 | tf_op jit(solution)/shard_map/ppermute | solution.py:931
  141.7 15.2 %collective-permute-start.34 = (f32[256,512]{1,0:T(8,128)S(1)}, f32[256,512]{1,0:T(8,128)S(1)}, u32[]{:S(2)}, u32[]{:S(2)}) collective-permute-start(f32[256,512]{1,0:T(8,128)S(1)} %get-tuple-element.387.refs_0_), channel_id=1, source_target_pairs={{0,1},{1,0},{2,3},{3,2},{4,5},{5,4},{6,7},{7,6},{8,24},{9,25},{10,... | collective-permute-start | bytes 1572872 | tf_op jit(solution)/shard_map/ppermute | solution.py:931
  147.0 9.7 %collective-permute-start.30 = (f32[80,512]{1,0:T(8,128)S(1)}, f32[80,512]{1,0:T(8,128)S(1)}, u32[]{:S(2)}, u32[]{:S(2)}) collective-permute-start(f32[80,512]{1,0:T(8,128)S(1)} %get-tuple-element.380), channel_id=1, source_target_pairs={{0,4},{1,5},{2,6},{3,7},{4,0},{5,1},{6,2},{7,3},{8,12},{9,13},{10,... | collective-permute-start | bytes 491528 | tf_op jit(solution)/shard_map/ppermute | solution.py:931
  148.9 13.0 %collective-permute-start.37 = (f32[128,512]{1,0:T(8,128)S(1)}, f32[128,512]{1,0:T(8,128)S(1)}, u32[]{:S(2)}, u32[]{:S(2)}) collective-permute-start(f32[128,512]{1,0:T(8,128)S(1)} %get-tuple-element.392.refs_0_), channel_id=1, source_target_pairs={{0,1},{1,0},{2,3},{3,2},{4,5},{5,4},{6,7},{7,6},{8,24},{9,25},{10,... | collective-permute-start | bytes 786440 | tf_op jit(solution)/shard_map/ppermute | solution.py:931
  157.0 14.9 %collective-permute-start.36 = (f32[512,512]{1,0:T(8,128)S(1)}, f32[512,512]{1,0:T(8,128)S(1)}, u32[]{:S(2)}, u32[]{:S(2)}) collective-permute-start(f32[512,512]{1,0:T(8,128)S(1)} %get-tuple-element.391.refs_0_), channel_id=1, source_target_pairs={{0,16},{1,17},{2,18},{3,19},{4,20},{5,21},{6,22},{7,23},{8,9},{9,8... | collective-permute-start | bytes 3145736 | tf_op jit(solution)/shard_map/ppermute | solution.py:931
  172.0 9.3 %collective-permute-start.41 = (f32[1024,512]{1,0:T(8,128)S(1)}, f32[1024,512]{1,0:T(8,128)S(1)}, u32[]{:S(2)}, u32[]{:S(2)}) collective-permute-start(f32[1024,512]{1,0:T(8,128)S(1)} %get-tuple-element.400.refs_0_), channel_id=1, source_target_pairs={{0,8},{1,9},{2,10},{3,11},{4,12},{5,13},{6,14},{7,15},{8,0},{9,1},... | collective-permute-start | bytes 6291464 | tf_op jit(solution)/shard_map/ppermute | solution.py:931
  172.1 9.0 %collective-permute-start.35 = (f32[128,512]{1,0:T(8,128)S(1)}, f32[128,512]{1,0:T(8,128)S(1)}, u32[]{:S(2)}, u32[]{:S(2)}) collective-permute-start(f32[128,512]{1,0:T(8,128)S(1)} %get-tuple-element.390.refs_0_), channel_id=1, source_target_pairs={{0,1},{1,0},{2,3},{3,2},{4,5},{5,4},{6,7},{7,6},{8,24},{9,25},{10,... | collective-permute-start | bytes 786440 | tf_op jit(solution)/shard_map/ppermute | solution.py:931
  174.4 9.0 %collective-permute-start.40 = (f32[1024,512]{1,0:T(8,128)S(1)}, f32[1024,512]{1,0:T(8,128)S(1)}, u32[]{:S(2)}, u32[]{:S(2)}) collective-permute-start(f32[1024,512]{1,0:T(8,128)S(1)} %get-tuple-element.399.refs_0_), channel_id=1, source_target_pairs={{0,8},{1,9},{2,10},{3,11},{4,12},{5,13},{6,14},{7,15},{8,0},{9,1},... | collective-permute-start | bytes 6291464 | tf_op jit(solution)/shard_map/ppermute | solution.py:931
  174.4 11.1 %collective-permute-start.39 = (f32[256,512]{1,0:T(8,128)S(1)}, f32[256,512]{1,0:T(8,128)S(1)}, u32[]{:S(2)}, u32[]{:S(2)}) collective-permute-start(f32[256,512]{1,0:T(8,128)S(1)} %get-tuple-element.398.refs_0_), channel_id=1, source_target_pairs={{0,16},{1,17},{2,18},{3,19},{4,20},{5,21},{6,22},{7,23},{8,9},{9,8... | collective-permute-start | bytes 1572872 | tf_op jit(solution)/shard_map/ppermute | solution.py:931
  181.1 9.2 %collective-permute-start.38 = (f32[256,512]{1,0:T(8,128)S(1)}, f32[256,512]{1,0:T(8,128)S(1)}, u32[]{:S(2)}, u32[]{:S(2)}) collective-permute-start(f32[256,512]{1,0:T(8,128)S(1)} %get-tuple-element.396.refs_0_), channel_id=1, source_target_pairs={{0,16},{1,17},{2,18},{3,19},{4,20},{5,21},{6,22},{7,23},{8,9},{9,8... | collective-permute-start | bytes 1572872 | tf_op jit(solution)/shard_map/ppermute | solution.py:931
  (40 other events, 169.6 us)
where the time goes:
time: 199 us; the launch traced here: 196 us
  waiting for transfers between devices  72.2 us (36%)
  Pallas kernels  69.2 us (35%)
  starting transfers between devices  51 us (26%)
    ppermute x36, waiting for transfers between devices, swap(): return lax.ppermute(array, ('batch', 'seq'), pairs)  70.1 us
    pallas_call x57, Pallas kernels, call(): pl.pallas_call(body, out_shape=shapes + (jax.ShapeDtypeStruct(TOKEN, f32)...  69.2 us
    ppermute x36, starting transfers between devices, swap(): return lax.ppermute(array, ('batch', 'seq'), pairs)  34.2 us
    ppermute x1, starting transfers between devices, rows_grad(): lax.ppermute(gfar[-1], 'seq', [(i, i ^ 1 << crossing - 1) for i in range(...  5.37 us
    ppermute x2, starting transfers between devices, coarser(): lax.ppermute(at.coarse_own, 'seq', [(i, i ^ 1 << bit) for i in range(seq_...  4.22 us
  transfers between devices with their start and end apart: 44, of which 23 were waited for; matrix products, arithmetic and copies ran while one was open for 0% of the time, Pallas kernels for 30%

commit v1 on v0

--- a/solution.py
+++ b/solution.py
@@ -22,10 +22,10 @@
 TOKEN = (8, 128)
 PLAN = (
     "first_norm", "project_qk", "project_v", "coarser", "rest_coarser", "local", "remote",
-    "outer0", "outer1", "inner0", "A", "inner1", "middle_grad", "B", "A", "pairs0", "pairs1", "A",
-    "rows_grad", "B", "A", "finer", "square0", "finer", "B", "C", "square1", "A", "C", "A", "B",
-    "C", "first_grad", "D", "A", "C", "B", "D", "D", "C", "B", "D", "A", "C", "D", "B", "D", "C",
-    "B", "D", "write_inner", "write_outer", "C", "D", "write_square0", "write_square1",
+    "outer0", "outer1", "inner0", "A", "inner1", "middle_grad", "B", "A", "pairs1", "pairs0", "A",
+    "rows_grad", "B", "A", "finer", "square0", "finer", "B", "C", "square1", "first_grad", "A",
+    "C", "B", "A", "D", "C", "A", "C", "D", "B", "D", "C", "B", "D", "C", "B", "D", "A", "B", "D",
+    "C", "write_outer", "D", "write_inner", "C", "D", "write_square0", "write_square1",
 )
 COST = 10**10
 INNER, OUTER, ODD, FIRST, LAST, CORE = range(6)

time: 199 us -> 194 us (0.975)
  waiting for transfers between devices: 72.2 us -> 58.8 us
  starting transfers between devices: 51 us -> 59.9 us
    ppermute x36, waiting for transfers between devices: 70.1 us -> 56.7 us  [swap(): return lax.ppermute(array, ('batch', 'seq'), pairs)]
    ppermute x36, starting transfers between devices: 34.2 us -> 43.1 us  [swap(): return lax.ppermute(array, ('batch', 'seq'), pairs)]
  transfers between devices with their start and end apart: 44 -> 44, of which waited for: 23 -> 16; matrix products, arithmetic and copies ran while one was open for 0% -> 0% of each run, Pallas kernels for 30% -> 31%
where the time goes in v1:
time: 194 us; the launch traced here: 191 us
  Pallas kernels  69.1 us (36%)
  starting transfers between devices  59.9 us (31%)
  waiting for transfers between devices  58.8 us (30%)
    pallas_call x57, Pallas kernels, call(): pl.pallas_call(body, out_shape=shapes + (jax.ShapeDtypeStruct(TOKEN, f32)...  69.1 us
    ppermute x36, waiting for transfers between devices, swap(): return lax.ppermute(array, ('batch', 'seq'), pairs)  56.7 us
    ppermute x36, starting transfers between devices, swap(): return lax.ppermute(array, ('batch', 'seq'), pairs)  43.1 us
    ppermute x1, starting transfers between devices, rows_grad(): lax.ppermute(gfar[-1], 'seq', [(i, i ^ 1 << crossing - 1) for i in range(...  5.36 us
    ppermute x2, starting transfers between devices, coarser(): lax.ppermute(at.coarse_own, 'seq', [(i, i ^ 1 << bit) for i in range(seq_...  4.22 us
  transfers between devices with their start and end apart: 44, of which 16 were waited for; matrix products, arithmetic and copies ran while one was open for 0% of the time, Pallas kernels for 31%

profile of v1, /device:TPU:0, one launch (start us, length us, event | category | flops | bytes accessed | tf_op | source)
XLA Modules:
  0.0 191.1 jit_solution(8257304533046135393)
XLA Ops:
  2.4 3.0 %collective-permute-start = (f32[2,32,512]{2,1,0:T(8,128)S(1)}, f32[2,32,512]{2,1,0:T(8,128)S(1)}, u32[]{:S(2)}, u32[]{:S(2)}) collective-permute-start(f32[2,32,512]{2,1,0:T(8,128)S(1)} %get-tuple-element.223.refs_0_), channel_id=1, source_target_pairs={{0,1},{1,0},{2,3},{3,2},{4,5},{5,4},{6,7},{7,6},{8,9},{9,8},{10,11... | collective-permute-start | bytes 393224 | tf_op jit(solution)/shard_map/ppermute | solution.py:1047
  5.5 2.6 %project_kernelqk.1 = (f32[512,512]{1,0:T(8,128)S(1)}, f32[512,512]{1,0:T(8,128)S(1)}, f32[512,512]{1,0:T(8,128)S(1)}, f32[512,512]{1,0:T(8,128)S(1)}, f32[8,128]{1,0:T(8,128)S(1)}) custom-call(f32[512,512]{1,0:T(8,128)S(1)} %get-tuple-element.224.refs_0_.refs_5_, f32[1,512]{1,0:T(1,128)S(1)} %bitcast.43, f32[1,512]{1,0:T(1,128)S(1)} %bitcast.37, ...), custom_call_target="tpu_custom_call" | custom-call | flops 10000000000 | tf_op jit(solution)/shard_map/project_kernelqk/pallas_call | solution.py:897
  14.0 2.6 %collective-permute-start.2 = (f32[2,16,512]{2,1,0:T(8,128)S(1)}, f32[2,16,512]{2,1,0:T(8,128)S(1)}, u32[]{:S(2)}, u32[]{:S(2)}) collective-permute-start(f32[2,16,512]{2,1,0:T(8,128)S(1)} %get-tuple-element.230), channel_id=1, source_target_pairs={{0,4},{1,5},{2,6},{3,7},{4,0},{5,1},{6,2},{7,3},{8,12},{9,13},{10,... | collective-permute-start | bytes 196616 | tf_op jit(solution)/shard_map/ppermute | solution.py:1077
  16.8 4.1 %local_kernel.1 = (f32[1024,256]{1,0:T(8,128)S(1)}, f32[16,256]{1,0:T(8,128)S(1)}, f32[1024,128]{1,0:T(8,128)S(1)}, f32[16,128]{1,0:T(8,128)S(1)}, f32[64,512]{1...) custom-call(f32[512,512]{1,0:T(8,128)S(1)} %get-tuple-element.231.refs_0_, ...), custom_call_target="tpu_custom_call" | custom-call | flops 10000000000 | tf_op jit(solution)/shard_map/local_kernel/pallas_call | solution.py:897
  21.0 4.1 %remote_kernel.1 = (f32[96,512]{1,0:T(8,128)S(1)}, f32[96,512]{1,0:T(8,128)S(1)}, f32[96,512]{1,0:T(8,128)S(1)}, f32[1024,256]{1,0:T(8,128)S(1)}, f32[16,256]{1,...) custom-call(f32[2,32,512]{2,1,0:T(8,128)S(1)} %collective-permute-do, ...), custom_call_target="tpu_custom_call" | custom-call | flops 10000000000 | tf_op jit(solution)/shard_map/remote_kernel/pallas_call | solution.py:897
  25.2 4.0 %outer_kernel0.1 = (f32[1024,512]{1,0:T(8,128)S(1)}, bf16[512,1024]{1,0:T(8,128)(2,1)S(1)}, bf16[512,1024]{1,0:T(8,128)(2,1)S(1)}, f32[512,1024]{1,0:T(8,128)S(1)}, f32[8,128]{1,0:T(8,128)S(1)}) custom-call(bf16[512,512]{1,0:T(8,128)(2,1)S(1)} %get-tuple-element.244.refs_0_, bf16[512,512]{1,0:T(8,128)(2,1)S(1)} %get-tuple-element.245.refs_1_, ...), custom_call_target="tpu_custom_call" | custom-call | flops 10000000000 | tf_op jit(solution)/shard_map/outer_kernel0/pallas_call | solution.py:897
  29.2 4.1 %outer_kernel1.1 = (f32[1024,512]{1,0:T(8,128)S(1)}, bf16[512,1024]{1,0:T(8,128)(2,1)S(1)}, bf16[512,1024]{1,0:T(8,128)(2,1)S(1)}, f32[512,1024]{1,0:T(8,128)S(1)}, f32[8,128]{1,0:T(8,128)S(1)}) custom-call(bf16[512,512]{1,0:T(8,128)(2,1)S(1)} %get-tuple-element.244.refs_0_, bf16[512,512]{1,0:T(8,128)(2,1)S(1)} %get-tuple-element.245.refs_1_, ...), custom_call_target="tpu_custom_call" | custom-call | flops 10000000000 | tf_op jit(solution)/shard_map/outer_kernel1/pallas_call | solution.py:897
  33.4 6.8 %inner_kernel0.1 = (f32[1024,512]{1,0:T(8,128)S(1)}, f32[1,1024]{1,0:T(1,128)S(1)}, f32[512,512]{1,0:T(8,128)S(1)}, f32[512,512]{1,0:T(8,128)S(1)}, f32[8,128]{1,0:T(8,128)S(1)}) custom-call(bf16[512,512]{1,0:T(8,128)(2,1)S(1)} %get-tuple-element.244.refs_0_, bf16[512,512]{1,0:T(8,128)(2,1)S(1)} %get-tuple-element.245.refs_1_, ...), custom_call_target="tpu_custom_call" | custom-call | flops 10000000000 | tf_op jit(solution)/shard_map/inner_kernel0/pallas_call | solution.py:897
  42.6 6.8 %inner_kernel1.1 = (f32[1024,512]{1,0:T(8,128)S(1)}, f32[1,1024]{1,0:T(1,128)S(1)}, f32[512,512]{1,0:T(8,128)}, f32[512,512]{1,0:T(8,128)S(1)}, f32[8,128]{1,0:T(8,128)S(1)}) custom-call(bf16[512,512]{1,0:T(8,128)(2,1)S(1)} %get-tuple-element.244.refs_0_, bf16[512,512]{1,0:T(8,128)(2,1)S(1)} %get-tuple-element.245.refs_1_, ...), custom_call_target="tpu_custom_call" | custom-call | flops 10000000000 | tf_op jit(solution)/shard_map/inner_kernel1/pallas_call | solution.py:897
  49.3 3.1 %middle_grad_kernel.1 = (f32[512,512]{1,0:T(8,128)S(1)}, f32[512,512]{1,0:T(8,128)S(1)}, f32[8,512]{1,0:T(8,128)S(1)}, f32[512,512]{1,0:T(8,128)S(1)}, f32[1024,...) custom-call(f32[512,512]{1,0:T(8,128)S(1)} %bitcast.25, ...), custom_call_target="tpu_custom_call" | custom-call | flops 10000000000 | tf_op jit(solution)/shard_map/middle_grad_kernel/pallas_call | solution.py:897
  53.2 2.6 %collective-permute-done.5.refs_1_ = f32[512,512]{1,0:T(8,128)S(1)} collective-permute-done((f32[512,512]{1,0:T(8,128)S(1)}, f32[512,512]{1,0:T(8,128)S(1)}, u32[]{:S(2)}, u32[]{:S(2)}) %collective-permute-start.5) | collective-permute-done | bytes 1048608 | tf_op jit(solution)/shard_map/ppermute | solution.py:931
  56.0 3.0 %collective-permute-start.7 = (f32[256,512]{1,0:T(8,128)S(1)}, f32[256,512]{1,0:T(8,128)S(1)}, u32[]{:S(2)}, u32[]{:S(2)}) collective-permute-start(f32[256,512]{1,0:T(8,128)S(1)} %get-tuple-element.305), channel_id=1, source_target_pairs={{0,1},{1,0},{2,3},{3,2},{4,5},{5,4},{6,7},{7,6},{8,24},{9,25},{10,... | collective-permute-start | bytes 1572872 | tf_op jit(solution)/shard_map/ppermute | solution.py:931
  59.0 5.7 %pairs_grad_kernel1.1 = (f32[512,256]{1,0:T(8,128)S(1)}, f32[512,256]{1,0:T(8,128)S(1)}, f32[512,256]{1,0:T(8,128)S(1)}, f32[160,256]{1,0:T(8,128)S(1)}, f32[160,256]{1,0:T(8,128)S(1)}, /*index=5*/f32[8,128]{1,0:T(8,128)S(1)}) custom-call(f32[512,512]{1,0:T(8,128)S(1)} %get-tuple-element.231.refs_0_, f32[512,512]{1,0:T(8,128)S(1)} %get-tuple-element.232.refs_1_, ...), custom_call_target="tpu_custom_call" | custom-call | flops 10000000000 | tf_op jit(solution)/shard_map/pairs_grad_kernel1/pallas_call | solution.py:897
  64.7 5.9 %pairs_grad_kernel0.1 = (f32[512,256]{1,0:T(8,128)S(1)}, f32[512,256]{1,0:T(8,128)S(1)}, f32[512,256]{1,0:T(8,128)S(1)}, f32[160,256]{1,0:T(8,128)S(1)}, f32[160,256]{1,0:T(8,128)S(1)}, /*index=5*/f32[8,128]{1,0:T(8,128)S(1)}) custom-call(f32[512,512]{1,0:T(8,128)S(1)} %get-tuple-element.231.refs_0_, f32[512,512]{1,0:T(8,128)S(1)} %get-tuple-element.232.refs_1_, ...), custom_call_target="tpu_custom_call" | custom-call | flops 10000000000 | tf_op jit(solution)/shard_map/pairs_grad_kernel0/pallas_call | solution.py:897
  73.6 3.7 %rows_grad_kernel.1 = (f32[16,512]{1,0:T(8,128)S(1)}, f32[512,512]{1,0:T(8,128)S(1)}, f32[2,16,512]{2,1,0:T(8,128)S(1)}, f32[2,16,512]{2,1,0:T(8,128)S(1)}, f32[...) custom-call(f32[512,512]{1,0:T(8,128)S(1)} %copy-done.27, ...), custom_call_target="tpu_custom_call" | custom-call | flops 10000000000 | tf_op jit(solution)/shard_map/rows_grad_kernel/pallas_call | solution.py:897
  78.0 5.4 %collective-permute-start.9 = (f32[2,16,512]{2,1,0:T(8,128)S(1)}, f32[2,16,512]{2,1,0:T(8,128)S(1)}, u32[]{:S(2)}, u32[]{:S(2)}) collective-permute-start(f32[2,16,512]{2,1,0:T(8,128)S(1)} %get-tuple-element.310), channel_id=1, source_target_pairs={{0,4},{1,5},{2,6},{3,7},{4,0},{5,1},{6,2},{7,3},{8,12},{9,13},{10,... | collective-permute-start | bytes 196616 | tf_op jit(solution)/shard_map/ppermute | solution.py:1192
  83.5 2.1 %collective-permute-start.15 = (f32[256,512]{1,0:T(8,128)S(1)}, f32[256,512]{1,0:T(8,128)S(1)}, u32[]{:S(2)}, u32[]{:S(2)}) collective-permute-start(f32[256,512]{1,0:T(8,128)S(1)} %get-tuple-element.333), channel_id=1, source_target_pairs={{0,1},{1,0},{2,3},{3,2},{4,5},{5,4},{6,7},{7,6},{8,24},{9,25},{10,... | collective-permute-start | bytes 1572872 | tf_op jit(solution)/shard_map/ppermute | solution.py:931
  88.3 2.6 %collective-permute-start.17 = (f32[128,512]{1,0:T(8,128)S(1)}, f32[128,512]{1,0:T(8,128)S(1)}, u32[]{:S(2)}, u32[]{:S(2)}) collective-permute-start(f32[128,512]{1,0:T(8,128)S(1)} %get-tuple-element.343), channel_id=1, source_target_pairs={{0,4},{1,5},{2,6},{3,7},{4,0},{5,1},{6,2},{7,3},{8,12},{9,13},{10,... | collective-permute-start | bytes 786440 | tf_op jit(solution)/shard_map/ppermute | solution.py:931
  95.9 2.1 %square_grad_kernel1.1 = (f32[512,512]{1,0:T(8,128)S(1)}, f32[512,512]{1,0:T(8,128)S(1)}, f32[8,128]{1,0:T(8,128)S(1)}) custom-call(f32[512,512]{1,0:T(8,128)S(1)} %copy-done.27, f32[64,512]{1,0:T(8,128)S(1)} %get-tuple-element.272.refs_1_, f32[96,512]{1,0:T(8,128)S(1)} %get-tuple-element.273.refs_2_, f32[1,512]{1,0:T(1,128)S(1)} %bitcast.48, ...), custom_call_target="tpu_custom_call" | custom-call | flops 10000000000 | tf_op jit(solution)/shard_map/square_grad_kernel1/pallas_call | solution.py:897
  101.6 5.7 %collective-permute-done.20.refs_1_ = f32[256,512]{1,0:T(8,128)S(1)} collective-permute-done((f32[256,512]{1,0:T(8,128)S(1)}, f32[256,512]{1,0:T(8,128)S(1)}, u32[]{:S(2)}, u32[]{:S(2)}) %collective-permute-start.20) | collective-permute-done | bytes 524320 | tf_op jit(solution)/shard_map/ppermute | solution.py:931
  108.2 2.1 %collective-permute-start.22 = (f32[128,512]{1,0:T(8,128)S(1)}, f32[128,512]{1,0:T(8,128)S(1)}, u32[]{:S(2)}, u32[]{:S(2)}) collective-permute-start(f32[128,512]{1,0:T(8,128)S(1)} %get-tuple-element.357), channel_id=1, source_target_pairs={{0,1},{1,0},{2,3},{3,2},{4,5},{5,4},{6,7},{7,6},{8,24},{9,25},{10,... | collective-permute-start | bytes 786440 | tf_op jit(solution)/shard_map/ppermute | solution.py:931
  111.6 2.2 %collective-permute-start.24 = (f32[256,512]{1,0:T(8,128)S(1)}, f32[256,512]{1,0:T(8,128)S(1)}, u32[]{:S(2)}, u32[]{:S(2)}) collective-permute-start(f32[256,512]{1,0:T(8,128)S(1)} %get-tuple-element.361.refs_0_), channel_id=1, source_target_pairs={{0,1},{1,0},{2,3},{3,2},{4,5},{5,4},{6,7},{7,6},{8,24},{9,25},{10,... | collective-permute-start | bytes 1572872 | tf_op jit(solution)/shard_map/ppermute | solution.py:931
  118.1 7.5 %collective-permute-done.24.refs_1_ = f32[256,512]{1,0:T(8,128)S(1)} collective-permute-done((f32[256,512]{1,0:T(8,128)S(1)}, f32[256,512]{1,0:T(8,128)S(1)}, u32[]{:S(2)}, u32[]{:S(2)}) %collective-permute-start.24) | collective-permute-done | bytes 524320 | tf_op jit(solution)/shard_map/ppermute | solution.py:931
  130.5 2.8 %collective-permute-start.28 = (f32[128,512]{1,0:T(8,128)S(1)}, f32[128,512]{1,0:T(8,128)S(1)}, u32[]{:S(2)}, u32[]{:S(2)}) collective-permute-start(f32[128,512]{1,0:T(8,128)S(1)} %get-tuple-element.373.refs_0_), channel_id=1, source_target_pairs={{0,2},{1,3},{2,0},{3,1},{4,6},{5,7},{6,4},{7,5},{8,10},{9,11},{10,... | collective-permute-start | bytes 786440 | tf_op jit(solution)/shard_map/ppermute | solution.py:931
  133.2 5.7 %collective-permute-done.25.refs_1_ = f32[144,512]{1,0:T(8,128)S(1)} collective-permute-done((f32[144,512]{1,0:T(8,128)S(1)}, f32[144,512]{1,0:T(8,128)S(1)}, u32[]{:S(2)}, u32[]{:S(2)}) %collective-permute-start.25) | collective-permute-done | bytes 294944 | tf_op jit(solution)/shard_map/ppermute | solution.py:931
  139.0 2.2 %collective-permute-start.32 = (f32[64,512]{1,0:T(8,128)S(1)}, f32[64,512]{1,0:T(8,128)S(1)}, u32[]{:S(2)}, u32[]{:S(2)}) collective-permute-start(f32[64,512]{1,0:T(8,128)S(1)} %get-tuple-element.382.refs_0_), channel_id=1, source_target_pairs={{0,2},{1,3},{2,0},{3,1},{4,6},{5,7},{6,4},{7,5},{8,10},{9,11},{10,... | collective-permute-start | bytes 393224 | tf_op jit(solution)/shard_map/ppermute | solution.py:931
  143.3 4.7 %collective-permute-done.27.refs_1_ = f32[80,512]{1,0:T(8,128)S(1)} collective-permute-done((f32[80,512]{1,0:T(8,128)S(1)}, f32[80,512]{1,0:T(8,128)S(1)}, u32[]{:S(2)}, u32[]{:S(2)}) %collective-permute-start.27) | collective-permute-done | bytes 163872 | tf_op jit(solution)/shard_map/ppermute | solution.py:931
  149.7 2.4 %collective-permute-start.38 = (f32[128,512]{1,0:T(8,128)S(1)}, f32[128,512]{1,0:T(8,128)S(1)}, u32[]{:S(2)}, u32[]{:S(2)}) collective-permute-start(f32[128,512]{1,0:T(8,128)S(1)} %get-tuple-element.394.refs_0_), channel_id=1, source_target_pairs={{0,1},{1,0},{2,3},{3,2},{4,5},{5,4},{6,7},{7,6},{8,24},{9,25},{10,... | collective-permute-start | bytes 786440 | tf_op jit(solution)/shard_map/ppermute | solution.py:931
  152.3 3.8 %collective-permute-done.30.refs_1_ = f32[80,512]{1,0:T(8,128)S(1)} collective-permute-done((f32[80,512]{1,0:T(8,128)S(1)}, f32[80,512]{1,0:T(8,128)S(1)}, u32[]{:S(2)}, u32[]{:S(2)}) %collective-permute-start.30) | collective-permute-done | bytes 163872 | tf_op jit(solution)/shard_map/ppermute | solution.py:931
  157.0 10.0 %collective-permute-done.34.refs_1_ = f32[512,512]{1,0:T(8,128)S(1)} collective-permute-done((f32[512,512]{1,0:T(8,128)S(1)}, f32[512,512]{1,0:T(8,128)S(1)}, u32[]{:S(2)}, u32[]{:S(2)}) %collective-permute-start.34) | collective-permute-done | bytes 1048608 | tf_op jit(solution)/shard_map/ppermute | solution.py:931
  171.0 5.4 %collective-permute-done.36.refs_1_ = f32[128,512]{1,0:T(8,128)S(1)} collective-permute-done((f32[128,512]{1,0:T(8,128)S(1)}, f32[128,512]{1,0:T(8,128)S(1)}, u32[]{:S(2)}, u32[]{:S(2)}) %collective-permute-start.36) | collective-permute-done | bytes 262176 | tf_op jit(solution)/shard_map/ppermute | solution.py:931
  179.3 6.5 %collective-permute-done.39.refs_1_ = f32[256,512]{1,0:T(8,128)S(1)} collective-permute-done((f32[256,512]{1,0:T(8,128)S(1)}, f32[256,512]{1,0:T(8,128)S(1)}, u32[]{:S(2)}, u32[]{:S(2)}) %collective-permute-start.39) | collective-permute-done | bytes 524320 | tf_op jit(solution)/shard_map/ppermute | solution.py:931
  (169 shorter events, 53.7 us)
Async XLA Ops:
  29.1 11.6 %collective-permute-start.4 = (f32[1024,512]{1,0:T(8,128)S(1)}, f32[1024,512]{1,0:T(8,128)S(1)}, u32[]{:S(2)}, u32[]{:S(2)}) collective-permute-start(f32[1024,512]{1,0:T(8,128)S(1)} %get-tuple-element.261), channel_id=1, source_target_pairs={{0,8},{1,9},{2,10},{3,11},{4,12},{5,13},{6,14},{7,15},{8,0},{9,1},... | collective-permute-start | bytes 6291464 | tf_op jit(solution)/shard_map/ppermute | solution.py:931
  40.2 12.2 %collective-permute-start.6 = (f32[1024,512]{1,0:T(8,128)S(1)}, f32[1024,512]{1,0:T(8,128)S(1)}, u32[]{:S(2)}, u32[]{:S(2)}) collective-permute-start(f32[1024,512]{1,0:T(8,128)S(1)} %get-tuple-element.286), channel_id=1, source_target_pairs={{0,8},{1,9},{2,10},{3,11},{4,12},{5,13},{6,14},{7,15},{8,0},{9,1},... | collective-permute-start | bytes 6291464 | tf_op jit(solution)/shard_map/ppermute | solution.py:931
  41.0 14.9 %collective-permute-start.5 = (f32[512,512]{1,0:T(8,128)S(1)}, f32[512,512]{1,0:T(8,128)S(1)}, u32[]{:S(2)}, u32[]{:S(2)}) collective-permute-start(f32[512,512]{1,0:T(8,128)S(1)} %get-tuple-element.284), channel_id=1, source_target_pairs={{0,16},{1,17},{2,18},{3,19},{4,20},{5,21},{6,22},{7,23},{8,9},{9,8... | collective-permute-start | bytes 3145736 | tf_op jit(solution)/shard_map/ppermute | solution.py:931
  52.6 30.7 %collective-permute-start.11 = (f32[512,512]{1,0:T(8,128)S(1)}, f32[512,512]{1,0:T(8,128)S(1)}, u32[]{:S(2)}, u32[]{:S(2)}) collective-permute-start(f32[512,512]{1,0:T(8,128)S(1)} %get-tuple-element.315), channel_id=1, source_target_pairs={{0,16},{1,17},{2,18},{3,19},{4,20},{5,21},{6,22},{7,23},{8,9},{9,8... | collective-permute-start | bytes 3145736 | tf_op jit(solution)/shard_map/ppermute | solution.py:931
  56.0 15.8 %collective-permute-start.7 = (f32[256,512]{1,0:T(8,128)S(1)}, f32[256,512]{1,0:T(8,128)S(1)}, u32[]{:S(2)}, u32[]{:S(2)}) collective-permute-start(f32[256,512]{1,0:T(8,128)S(1)} %get-tuple-element.305), channel_id=1, source_target_pairs={{0,1},{1,0},{2,3},{3,2},{4,5},{5,4},{6,7},{7,6},{8,24},{9,25},{10,... | collective-permute-start | bytes 1572872 | tf_op jit(solution)/shard_map/ppermute | solution.py:931
  71.9 13.7 %collective-permute-start.10 = (f32[128,512]{1,0:T(8,128)S(1)}, f32[128,512]{1,0:T(8,128)S(1)}, u32[]{:S(2)}, u32[]{:S(2)}) collective-permute-start(f32[128,512]{1,0:T(8,128)S(1)} %get-tuple-element.313), channel_id=1, source_target_pairs={{0,2},{1,3},{2,0},{3,1},{4,6},{5,7},{6,4},{7,5},{8,10},{9,11},{10,... | collective-permute-start | bytes 786440 | tf_op jit(solution)/shard_map/ppermute | solution.py:931
  77.3 8.4 %collective-permute-start.8 = (f32[2,16,512]{2,1,0:T(8,128)S(1)}, f32[2,16,512]{2,1,0:T(8,128)S(1)}, u32[]{:S(2)}, u32[]{:S(2)}) collective-permute-start(f32[2,16,512]{2,1,0:T(8,128)S(1)} %get-tuple-element.309), channel_id=1, source_target_pairs={{1,2},{2,1},{3,4},{4,3},{5,6},{6,5},{9,10},{10,9},{11,12},{12,11},... | collective-permute-start | bytes 196616 | tf_op jit(solution)/shard_map/ppermute | solution.py:1189
  78.0 8.2 %collective-permute-start.9 = (f32[2,16,512]{2,1,0:T(8,128)S(1)}, f32[2,16,512]{2,1,0:T(8,128)S(1)}, u32[]{:S(2)}, u32[]{:S(2)}) collective-permute-start(f32[2,16,512]{2,1,0:T(8,128)S(1)} %get-tuple-element.310), channel_id=1, source_target_pairs={{0,4},{1,5},{2,6},{3,7},{4,0},{5,1},{6,2},{7,3},{8,12},{9,13},{10,... | collective-permute-start | bytes 196616 | tf_op jit(solution)/shard_map/ppermute | solution.py:1192
  83.5 10.4 %collective-permute-start.15 = (f32[256,512]{1,0:T(8,128)S(1)}, f32[256,512]{1,0:T(8,128)S(1)}, u32[]{:S(2)}, u32[]{:S(2)}) collective-permute-start(f32[256,512]{1,0:T(8,128)S(1)} %get-tuple-element.333), channel_id=1, source_target_pairs={{0,1},{1,0},{2,3},{3,2},{4,5},{5,4},{6,7},{7,6},{8,24},{9,25},{10,... | collective-permute-start | bytes 1572872 | tf_op jit(solution)/shard_map/ppermute | solution.py:931
  88.3 12.9 %collective-permute-start.17 = (f32[128,512]{1,0:T(8,128)S(1)}, f32[128,512]{1,0:T(8,128)S(1)}, u32[]{:S(2)}, u32[]{:S(2)}) collective-permute-start(f32[128,512]{1,0:T(8,128)S(1)} %get-tuple-element.343), channel_id=1, source_target_pairs={{0,4},{1,5},{2,6},{3,7},{4,0},{5,1},{6,2},{7,3},{8,12},{9,13},{10,... | collective-permute-start | bytes 786440 | tf_op jit(solution)/shard_map/ppermute | solution.py:931
  94.0 13.4 %collective-permute-start.19 = (f32[128,512]{1,0:T(8,128)S(1)}, f32[128,512]{1,0:T(8,128)S(1)}, u32[]{:S(2)}, u32[]{:S(2)}) collective-permute-start(f32[128,512]{1,0:T(8,128)S(1)} %get-tuple-element.347), channel_id=1, source_target_pairs={{0,2},{1,3},{2,0},{3,1},{4,6},{5,7},{6,4},{7,5},{8,10},{9,11},{10,... | collective-permute-start | bytes 786440 | tf_op jit(solution)/shard_map/ppermute | solution.py:931
  98.1 9.2 %collective-permute-start.20 = (f32[256,512]{1,0:T(8,128)S(1)}, f32[256,512]{1,0:T(8,128)S(1)}, u32[]{:S(2)}, u32[]{:S(2)}) collective-permute-start(f32[256,512]{1,0:T(8,128)S(1)} %get-tuple-element.349), channel_id=1, source_target_pairs={{0,16},{1,17},{2,18},{3,19},{4,20},{5,21},{6,22},{7,23},{8,9},{9,8... | collective-permute-start | bytes 1572872 | tf_op jit(solution)/shard_map/ppermute | solution.py:931
  101.3 10.3 %collective-permute-start.18 = (f32[128,512]{1,0:T(8,128)S(1)}, f32[128,512]{1,0:T(8,128)S(1)}, u32[]{:S(2)}, u32[]{:S(2)}) collective-permute-start(f32[128,512]{1,0:T(8,128)S(1)} %get-tuple-element.345.refs_0_), channel_id=1, source_target_pairs={{0,2},{1,3},{2,0},{3,1},{4,6},{5,7},{6,4},{7,5},{8,10},{9,11},{10,... | collective-permute-start | bytes 786440 | tf_op jit(solution)/shard_map/ppermute | solution.py:931
  101.6 12.3 %collective-permute-start.16 = (f32[512,512]{1,0:T(8,128)S(1)}, f32[512,512]{1,0:T(8,128)S(1)}, u32[]{:S(2)}, u32[]{:S(2)}) collective-permute-start(f32[512,512]{1,0:T(8,128)S(1)} %get-tuple-element.340), channel_id=1, source_target_pairs={{0,8},{1,9},{2,10},{3,11},{4,12},{5,13},{6,14},{7,15},{8,0},{9,1},... | collective-permute-start | bytes 3145736 | tf_op jit(solution)/shard_map/ppermute | solution.py:931
  107.5 23.0 %collective-permute-start.26 = (f32[128,512]{1,0:T(8,128)S(1)}, f32[128,512]{1,0:T(8,128)S(1)}, u32[]{:S(2)}, u32[]{:S(2)}) collective-permute-start(f32[128,512]{1,0:T(8,128)S(1)} %get-tuple-element.368), channel_id=1, source_target_pairs={{0,4},{1,5},{2,6},{3,7},{4,0},{5,1},{6,2},{7,3},{8,12},{9,13},{10,... | collective-permute-start | bytes 786440 | tf_op jit(solution)/shard_map/ppermute | solution.py:931
  111.6 14.0 %collective-permute-start.24 = (f32[256,512]{1,0:T(8,128)S(1)}, f32[256,512]{1,0:T(8,128)S(1)}, u32[]{:S(2)}, u32[]{:S(2)}) collective-permute-start(f32[256,512]{1,0:T(8,128)S(1)} %get-tuple-element.361.refs_0_), channel_id=1, source_target_pairs={{0,1},{1,0},{2,3},{3,2},{4,5},{5,4},{6,7},{7,6},{8,24},{9,25},{10,... | collective-permute-start | bytes 1572872 | tf_op jit(solution)/shard_map/ppermute | solution.py:931
  114.7 13.0 %collective-permute-start.23 = (f32[64,512]{1,0:T(8,128)S(1)}, f32[64,512]{1,0:T(8,128)S(1)}, u32[]{:S(2)}, u32[]{:S(2)}) collective-permute-start(f32[64,512]{1,0:T(8,128)S(1)} %get-tuple-element.360), channel_id=1, source_target_pairs={{0,2},{1,3},{2,0},{3,1},{4,6},{5,7},{6,4},{7,5},{8,10},{9,11},{10,... | collective-permute-start | bytes 393224 | tf_op jit(solution)/shard_map/ppermute | solution.py:931
  116.6 12.2 %collective-permute-start.21 = (f32[272,512]{1,0:T(8,128)S(1)}, f32[272,512]{1,0:T(8,128)S(1)}, u32[]{:S(2)}, u32[]{:S(2)}) collective-permute-start(f32[272,512]{1,0:T(8,128)S(1)} %get-tuple-element.355), channel_id=1, source_target_pairs={{0,16},{1,17},{2,18},{3,19},{4,20},{5,21},{6,22},{7,23},{8,9},{9,8... | collective-permute-start | bytes 1671176 | tf_op jit(solution)/shard_map/ppermute | solution.py:931
  125.7 31.1 %collective-permute-start.35 = (f32[512,512]{1,0:T(8,128)S(1)}, f32[512,512]{1,0:T(8,128)S(1)}, u32[]{:S(2)}, u32[]{:S(2)}) collective-permute-start(f32[512,512]{1,0:T(8,128)S(1)} %get-tuple-element.388.refs_0_), channel_id=1, source_target_pairs={{0,16},{1,17},{2,18},{3,19},{4,20},{5,21},{6,22},{7,23},{8,9},{9,8... | collective-permute-start | bytes 3145736 | tf_op jit(solution)/shard_map/ppermute | solution.py:931
  127.7 11.2 %collective-permute-start.29 = (f32[64,512]{1,0:T(8,128)S(1)}, f32[64,512]{1,0:T(8,128)S(1)}, u32[]{:S(2)}, u32[]{:S(2)}) collective-permute-start(f32[64,512]{1,0:T(8,128)S(1)} %get-tuple-element.375), channel_id=1, source_target_pairs={{0,4},{1,5},{2,6},{3,7},{4,0},{5,1},{6,2},{7,3},{8,12},{9,13},{10,... | collective-permute-start | bytes 393224 | tf_op jit(solution)/shard_map/ppermute | solution.py:931
  128.9 10.0 %collective-permute-start.25 = (f32[144,512]{1,0:T(8,128)S(1)}, f32[144,512]{1,0:T(8,128)S(1)}, u32[]{:S(2)}, u32[]{:S(2)}) collective-permute-start(f32[144,512]{1,0:T(8,128)S(1)} %get-tuple-element.366), channel_id=1, source_target_pairs={{0,1},{1,0},{2,3},{3,2},{4,5},{5,4},{6,7},{7,6},{8,24},{9,25},{10,... | collective-permute-start | bytes 884744 | tf_op jit(solution)/shard_map/ppermute | solution.py:931
  130.5 10.8 %collective-permute-start.28 = (f32[128,512]{1,0:T(8,128)S(1)}, f32[128,512]{1,0:T(8,128)S(1)}, u32[]{:S(2)}, u32[]{:S(2)}) collective-permute-start(f32[128,512]{1,0:T(8,128)S(1)} %get-tuple-element.373.refs_0_), channel_id=1, source_target_pairs={{0,2},{1,3},{2,0},{3,1},{4,6},{5,7},{6,4},{7,5},{8,10},{9,11},{10,... | collective-permute-start | bytes 786440 | tf_op jit(solution)/shard_map/ppermute | solution.py:931
  139.0 10.7 %collective-permute-start.32 = (f32[64,512]{1,0:T(8,128)S(1)}, f32[64,512]{1,0:T(8,128)S(1)}, u32[]{:S(2)}, u32[]{:S(2)}) collective-permute-start(f32[64,512]{1,0:T(8,128)S(1)} %get-tuple-element.382.refs_0_), channel_id=1, source_target_pairs={{0,2},{1,3},{2,0},{3,1},{4,6},{5,7},{6,4},{7,5},{8,10},{9,11},{10,... | collective-permute-start | bytes 393224 | tf_op jit(solution)/shard_map/ppermute | solution.py:931
  141.3 10.7 %collective-permute-start.31 = (f32[256,512]{1,0:T(8,128)S(1)}, f32[256,512]{1,0:T(8,128)S(1)}, u32[]{:S(2)}, u32[]{:S(2)}) collective-permute-start(f32[256,512]{1,0:T(8,128)S(1)} %get-tuple-element.381.refs_0_), channel_id=1, source_target_pairs={{0,1},{1,0},{2,3},{3,2},{4,5},{5,4},{6,7},{7,6},{8,24},{9,25},{10,... | collective-permute-start | bytes 1572872 | tf_op jit(solution)/shard_map/ppermute | solution.py:931
  149.7 18.0 %collective-permute-start.38 = (f32[128,512]{1,0:T(8,128)S(1)}, f32[128,512]{1,0:T(8,128)S(1)}, u32[]{:S(2)}, u32[]{:S(2)}) collective-permute-start(f32[128,512]{1,0:T(8,128)S(1)} %get-tuple-element.394.refs_0_), channel_id=1, source_target_pairs={{0,1},{1,0},{2,3},{3,2},{4,5},{5,4},{6,7},{7,6},{8,24},{9,25},{10,... | collective-permute-start | bytes 786440 | tf_op jit(solution)/shard_map/ppermute | solution.py:931
  152.2 14.9 %collective-permute-start.34 = (f32[512,512]{1,0:T(8,128)S(1)}, f32[512,512]{1,0:T(8,128)S(1)}, u32[]{:S(2)}, u32[]{:S(2)}) collective-permute-start(f32[512,512]{1,0:T(8,128)S(1)} %get-tuple-element.387.refs_0_), channel_id=1, source_target_pairs={{0,16},{1,17},{2,18},{3,19},{4,20},{5,21},{6,22},{7,23},{8,9},{9,8... | collective-permute-start | bytes 3145736 | tf_op jit(solution)/shard_map/ppermute | solution.py:931
  156.1 11.1 %collective-permute-start.33 = (f32[64,512]{1,0:T(8,128)S(1)}, f32[64,512]{1,0:T(8,128)S(1)}, u32[]{:S(2)}, u32[]{:S(2)}) collective-permute-start(f32[64,512]{1,0:T(8,128)S(1)} %get-tuple-element.386.refs_0_), channel_id=1, source_target_pairs={{0,2},{1,3},{2,0},{3,1},{4,6},{5,7},{6,4},{7,5},{8,10},{9,11},{10,... | collective-permute-start | bytes 393224 | tf_op jit(solution)/shard_map/ppermute | solution.py:931
  157.0 12.0 %collective-permute-start.37 = (f32[1024,512]{1,0:T(8,128)S(1)}, f32[1024,512]{1,0:T(8,128)S(1)}, u32[]{:S(2)}, u32[]{:S(2)}) collective-permute-start(f32[1024,512]{1,0:T(8,128)S(1)} %get-tuple-element.393.refs_0_), channel_id=1, source_target_pairs={{0,8},{1,9},{2,10},{3,11},{4,12},{5,13},{6,14},{7,15},{8,0},{9,1},... | collective-permute-start | bytes 6291464 | tf_op jit(solution)/shard_map/ppermute | solution.py:931
  167.2 9.2 %collective-permute-start.36 = (f32[128,512]{1,0:T(8,128)S(1)}, f32[128,512]{1,0:T(8,128)S(1)}, u32[]{:S(2)}, u32[]{:S(2)}) collective-permute-start(f32[128,512]{1,0:T(8,128)S(1)} %get-tuple-element.392.refs_0_), channel_id=1, source_target_pairs={{0,1},{1,0},{2,3},{3,2},{4,5},{5,4},{6,7},{7,6},{8,24},{9,25},{10,... | collective-permute-start | bytes 786440 | tf_op jit(solution)/shard_map/ppermute | solution.py:931
  167.7 8.9 %collective-permute-start.41 = (f32[1024,512]{1,0:T(8,128)S(1)}, f32[1024,512]{1,0:T(8,128)S(1)}, u32[]{:S(2)}, u32[]{:S(2)}) collective-permute-start(f32[1024,512]{1,0:T(8,128)S(1)} %get-tuple-element.401.refs_0_), channel_id=1, source_target_pairs={{0,8},{1,9},{2,10},{3,11},{4,12},{5,13},{6,14},{7,15},{8,0},{9,1},... | collective-permute-start | bytes 6291464 | tf_op jit(solution)/shard_map/ppermute | solution.py:931
  167.8 10.9 %collective-permute-start.40 = (f32[256,512]{1,0:T(8,128)S(1)}, f32[256,512]{1,0:T(8,128)S(1)}, u32[]{:S(2)}, u32[]{:S(2)}) collective-permute-start(f32[256,512]{1,0:T(8,128)S(1)} %get-tuple-element.400.refs_0_), channel_id=1, source_target_pairs={{0,16},{1,17},{2,18},{3,19},{4,20},{5,21},{6,22},{7,23},{8,9},{9,8... | collective-permute-start | bytes 1572872 | tf_op jit(solution)/shard_map/ppermute | solution.py:931
  176.5 9.2 %collective-permute-start.39 = (f32[256,512]{1,0:T(8,128)S(1)}, f32[256,512]{1,0:T(8,128)S(1)}, u32[]{:S(2)}, u32[]{:S(2)}) collective-permute-start(f32[256,512]{1,0:T(8,128)S(1)} %get-tuple-element.398.refs_0_), channel_id=1, source_target_pairs={{0,16},{1,17},{2,18},{3,19},{4,20},{5,21},{6,22},{7,23},{8,9},{9,8... | collective-permute-start | bytes 1572872 | tf_op jit(solution)/shard_map/ppermute | solution.py:931
  (40 other events, 172.7 us)

commit v2 on v1

--- a/solution.py
+++ b/solution.py
@@ -22,11 +22,12 @@
 TOKEN = (8, 128)
 PLAN = (
     "first_norm", "project_qk", "project_v", "coarser", "rest_coarser", "local", "remote",
-    "outer0", "outer1", "inner0", "A", "inner1", "middle_grad", "B", "A", "pairs1", "pairs0", "A",
-    "rows_grad", "B", "A", "finer", "square0", "finer", "B", "C", "square1", "first_grad", "A",
-    "C", "B", "A", "D", "C", "A", "C", "D", "B", "D", "C", "B", "D", "C", "B", "D", "A", "B", "D",
-    "C", "write_outer", "D", "write_inner", "C", "D", "write_square0", "write_square1",
+    "outer0", "outer1", "inner0", "A", "inner1", "B", "middle_grad", "pairs0", "square0", "B",
+    "pairs1", "A", "B", "rows_grad", "B", "C", "A", "square1", "A", "finer", "D", "C", "B",
+    "finer", "C", "D", "B", "A", "D", "C", "A", "C", "first_grad", "D", "A", "C", "B", "C", "D",
+    "D", "B", "D", "C", "A", "write_inner", "D", "write_square0", "write_outer", "write_square1",
 )
+EARLY = "A"
 COST = 10**10
 INNER, OUTER, ODD, FIRST, LAST, CORE = range(6)
 
@@ -918,6 +919,7 @@
         wide = [(0, bit) for bit in range(1, across)]
         tail = [(1, bit) for bit in range(1, along)]
         self.steps = list(zip(wide + [(1, 0)] + tail, [(1, 0)] + wide + tail))
+        self.early = [(tail[0], tail[0])] + [step for step in self.steps if step[0] != tail[0]]
         self.core = ((0, 0), (0, 0))
 
     def swap(self, array, step):
@@ -930,11 +932,11 @@
                 pairs.append((batch * seq_count + seq, other[0] * seq_count + other[1]))
         return lax.ppermute(array, ("batch", "seq"), pairs)
 
-    def chunk(self, call, place, slot, kept, got, extra=None):
+    def chunk(self, call, place, steps, slot, kept, got, extra=None):
         size, width = kept.shape
         more = 0 if extra is None else extra.shape[0]
         keep = kept
-        for index, step in enumerate(self.steps):
+        for index, step in enumerate(steps):
             fresh = extra is not None and index == 0
             mode = "fresh" if fresh else extra is not None
             keep, send = call(
@@ -944,7 +946,7 @@
             )
             size //= 2
             got = self.swap(send, step)
-            if index + 2 == len(self.steps):
+            if index + 2 == len(steps):
                 break
             yield
         yield
@@ -952,15 +954,15 @@
             functools.partial(share_kernel, size, more),
             [(size + more, width)] * 2, [place, keep, got],
         )
-        got = self.swap(send, self.steps[-1])
+        got = self.swap(send, steps[-1])
         yield
         own = call(
             functools.partial(fold_kernel, None, size, extra is not None),
             [(size, width)] + ([(more, width)] if more else []), [place, keep, got],
         )
         own, rest = own[0], own[1:]
-        for index in range(len(self.steps) - 2, -1, -1):
-            got = self.swap(own, self.steps[index])
+        for index in range(len(steps) - 2, -1, -1):
+            got = self.swap(own, steps[index])
             yield
             last = list(rest) if index == 0 else []
             (own,) = call(
@@ -1005,7 +1007,7 @@
     everywhere = Everywhere(batch_count, seq_count)
     seq_slot = CORE + 1
     step_slot = seq_slot + crossing
-    place = Here(span, seq_count, everywhere.steps)
+    place = Here(span, seq_count, everywhere.steps + everywhere.early)
     inner_pairs = [(i, i ^ 1) for i in range(seq_count)]
     outer_pairs = [
         (i, j)
@@ -1029,9 +1031,12 @@
         if name not in sums:
             turns[name] = 0
             extra = at.vec if name == "D" else None
+            early = name in EARLY
+            steps = everywhere.early if early else everywhere.steps
             sums[name] = Run(
                 everywhere.chunk(
-                    lambda *rest: call(*rest, name + str(turns[name])), place, step_slot, at.kept[name], at.got[name],
+                    lambda *rest: call(*rest, name + str(turns[name])), place, steps,
+                    step_slot + early * len(steps), at.kept[name], at.got[name],
                     extra,
                 )
             )

time: 194 us -> 183 us (0.943)
  waiting for transfers between devices: 58.8 us -> 46.8 us
    ppermute x36, waiting for transfers between devices: 56.7 us -> 44.8 us  [swap(): return lax.ppermute(array, ('batch', 'seq'), pairs)]
  transfers between devices with their start and end apart: 44 -> 44, of which waited for: 16 -> 19; matrix products, arithmetic and copies ran while one was open for 0% -> 0% of each run, Pallas kernels for 31% -> 33%
where the time goes in v2:
time: 183 us; the launch traced here: 180 us
  Pallas kernels  69.6 us (38%)
  starting transfers between devices  59.8 us (33%)
  waiting for transfers between devices  46.8 us (26%)
  between operations  1.87 us (1%)
    pallas_call x57, Pallas kernels, call(): pl.pallas_call(body, out_shape=shapes + (jax.ShapeDtypeStruct(TOKEN, f32)...  69.6 us
    ppermute x36, waiting for transfers between devices, swap(): return lax.ppermute(array, ('batch', 'seq'), pairs)  44.8 us
    ppermute x36, starting transfers between devices, swap(): return lax.ppermute(array, ('batch', 'seq'), pairs)  42.4 us
    ppermute x1, starting transfers between devices, rows_grad(): lax.ppermute(gfar[-1], 'seq', [(i, i ^ 1 << crossing - 1) for i in range(...  4.79 us
    ppermute x2, starting transfers between devices, coarser(): lax.ppermute(at.coarse_own, 'seq', [(i, i ^ 1 << bit) for i in range(seq_...  4.22 us
  transfers between devices with their start and end apart: 44, of which 19 were waited for; matrix products, arithmetic and copies ran while one was open for 0% of the time, Pallas kernels for 33%

profile of v2, /device:TPU:0, one launch (start us, length us, event | category | flops | bytes accessed | tf_op | source)
XLA Modules:
  0.0 179.8 jit_solution(5112961217140829282)
XLA Ops:
  2.4 3.0 %collective-permute-start = (f32[2,32,512]{2,1,0:T(8,128)S(1)}, f32[2,32,512]{2,1,0:T(8,128)S(1)}, u32[]{:S(2)}, u32[]{:S(2)}) collective-permute-start(f32[2,32,512]{2,1,0:T(8,128)S(1)} %get-tuple-element.223.refs_0_), channel_id=1, source_target_pairs={{0,1},{1,0},{2,3},{3,2},{4,5},{5,4},{6,7},{7,6},{8,9},{9,8},{10,11... | collective-permute-start | bytes 393224 | tf_op jit(solution)/shard_map/ppermute | solution.py:1052
  5.4 2.6 %project_kernelqk.1 = (f32[512,512]{1,0:T(8,128)S(1)}, f32[512,512]{1,0:T(8,128)S(1)}, f32[512,512]{1,0:T(8,128)S(1)}, f32[512,512]{1,0:T(8,128)S(1)}, f32[8,128]{1,0:T(8,128)S(1)}) custom-call(f32[512,512]{1,0:T(8,128)S(1)} %get-tuple-element.224.refs_0_.refs_5_, f32[1,512]{1,0:T(1,128)S(1)} %bitcast.43, f32[1,512]{1,0:T(1,128)S(1)} %bitcast.37, ...), custom_call_target="tpu_custom_call" | custom-call | flops 10000000000 | tf_op jit(solution)/shard_map/project_kernelqk/pallas_call | solution.py:898
  14.0 2.6 %collective-permute-start.2 = (f32[2,16,512]{2,1,0:T(8,128)S(1)}, f32[2,16,512]{2,1,0:T(8,128)S(1)}, u32[]{:S(2)}, u32[]{:S(2)}) collective-permute-start(f32[2,16,512]{2,1,0:T(8,128)S(1)} %get-tuple-element.230), channel_id=1, source_target_pairs={{0,4},{1,5},{2,6},{3,7},{4,0},{5,1},{6,2},{7,3},{8,12},{9,13},{10,... | collective-permute-start | bytes 196616 | tf_op jit(solution)/shard_map/ppermute | solution.py:1082
  16.8 4.2 %local_kernel.1 = (f32[1024,256]{1,0:T(8,128)S(1)}, f32[16,256]{1,0:T(8,128)S(1)}, f32[1024,128]{1,0:T(8,128)S(1)}, f32[16,128]{1,0:T(8,128)S(1)}, f32[64,512]{1...) custom-call(f32[512,512]{1,0:T(8,128)S(1)} %get-tuple-element.231.refs_0_, ...), custom_call_target="tpu_custom_call" | custom-call | flops 10000000000 | tf_op jit(solution)/shard_map/local_kernel/pallas_call | solution.py:898
  21.1 4.2 %remote_kernel.1 = (f32[96,512]{1,0:T(8,128)S(1)}, f32[96,512]{1,0:T(8,128)S(1)}, f32[96,512]{1,0:T(8,128)S(1)}, f32[1024,256]{1,0:T(8,128)S(1)}, f32[16,256]{1,...) custom-call(f32[2,32,512]{2,1,0:T(8,128)S(1)} %collective-permute-do, ...), custom_call_target="tpu_custom_call" | custom-call | flops 10000000000 | tf_op jit(solution)/shard_map/remote_kernel/pallas_call | solution.py:898
  25.3 4.0 %outer_kernel0.1 = (f32[1024,512]{1,0:T(8,128)S(1)}, bf16[512,1024]{1,0:T(8,128)(2,1)S(1)}, bf16[512,1024]{1,0:T(8,128)(2,1)S(1)}, f32[512,1024]{1,0:T(8,128)S(1)}, f32[8,128]{1,0:T(8,128)S(1)}) custom-call(bf16[512,512]{1,0:T(8,128)(2,1)S(1)} %get-tuple-element.244.refs_0_, bf16[512,512]{1,0:T(8,128)(2,1)S(1)} %get-tuple-element.245.refs_1_, ...), custom_call_target="tpu_custom_call" | custom-call | flops 10000000000 | tf_op jit(solution)/shard_map/outer_kernel0/pallas_call | solution.py:898
  29.3 4.1 %outer_kernel1.1 = (f32[1024,512]{1,0:T(8,128)S(1)}, bf16[512,1024]{1,0:T(8,128)(2,1)S(1)}, bf16[512,1024]{1,0:T(8,128)(2,1)S(1)}, f32[512,1024]{1,0:T(8,128)S(1)}, f32[8,128]{1,0:T(8,128)S(1)}) custom-call(bf16[512,512]{1,0:T(8,128)(2,1)S(1)} %get-tuple-element.244.refs_0_, bf16[512,512]{1,0:T(8,128)(2,1)S(1)} %get-tuple-element.245.refs_1_, ...), custom_call_target="tpu_custom_call" | custom-call | flops 10000000000 | tf_op jit(solution)/shard_map/outer_kernel1/pallas_call | solution.py:898
  33.5 6.8 %inner_kernel0.1 = (f32[1024,512]{1,0:T(8,128)S(1)}, f32[1,1024]{1,0:T(1,128)S(1)}, f32[512,512]{1,0:T(8,128)S(1)}, f32[512,512]{1,0:T(8,128)S(1)}, f32[8,128]{1,0:T(8,128)S(1)}) custom-call(bf16[512,512]{1,0:T(8,128)(2,1)S(1)} %get-tuple-element.244.refs_0_, bf16[512,512]{1,0:T(8,128)(2,1)S(1)} %get-tuple-element.245.refs_1_, ...), custom_call_target="tpu_custom_call" | custom-call | flops 10000000000 | tf_op jit(solution)/shard_map/inner_kernel0/pallas_call | solution.py:898
  41.1 2.4 %collective-permute-start.8 = (f32[512,512]{1,0:T(8,128)S(1)}, f32[512,512]{1,0:T(8,128)S(1)}, u32[]{:S(2)}, u32[]{:S(2)}) collective-permute-start(f32[512,512]{1,0:T(8,128)S(1)} %get-tuple-element.309), channel_id=1, source_target_pairs={{0,2},{1,3},{2,0},{3,1},{4,6},{5,7},{6,4},{7,5},{8,10},{9,11},{10,... | collective-permute-start | bytes 3145736 | tf_op jit(solution)/shard_map/ppermute | solution.py:933
  43.5 6.8 %inner_kernel1.1 = (f32[1024,512]{1,0:T(8,128)S(1)}, f32[1,1024]{1,0:T(1,128)S(1)}, f32[512,512]{1,0:T(8,128)}, f32[512,512]{1,0:T(8,128)S(1)}, f32[8,128]{1,0:T(8,128)S(1)}) custom-call(bf16[512,512]{1,0:T(8,128)(2,1)S(1)} %get-tuple-element.244.refs_0_, bf16[512,512]{1,0:T(8,128)(2,1)S(1)} %get-tuple-element.245.refs_1_, ...), custom_call_target="tpu_custom_call" | custom-call | flops 10000000000 | tf_op jit(solution)/shard_map/inner_kernel1/pallas_call | solution.py:898
  52.1 3.2 %middle_grad_kernel.1 = (f32[512,512]{1,0:T(8,128)S(1)}, f32[512,512]{1,0:T(8,128)S(1)}, f32[8,512]{1,0:T(8,128)S(1)}, f32[512,512]{1,0:T(8,128)S(1)}, f32[1024,...) custom-call(f32[512,512]{1,0:T(8,128)S(1)} %bitcast.25, ...), custom_call_target="tpu_custom_call" | custom-call | flops 10000000000 | tf_op jit(solution)/shard_map/middle_grad_kernel/pallas_call | solution.py:898
  55.2 5.7 %pairs_grad_kernel0.1 = (f32[512,256]{1,0:T(8,128)S(1)}, f32[512,256]{1,0:T(8,128)S(1)}, f32[512,256]{1,0:T(8,128)S(1)}, f32[160,256]{1,0:T(8,128)S(1)}, f32[160,256]{1,0:T(8,128)S(1)}, /*index=5*/f32[8,128]{1,0:T(8,128)S(1)}) custom-call(f32[512,512]{1,0:T(8,128)S(1)} %get-tuple-element.231.refs_0_, f32[512,512]{1,0:T(8,128)S(1)} %get-tuple-element.232.refs_1_, ...), custom_call_target="tpu_custom_call" | custom-call | flops 10000000000 | tf_op jit(solution)/shard_map/pairs_grad_kernel0/pallas_call | solution.py:898
  61.0 2.1 %square_grad_kernel0.1 = (f32[512,512]{1,0:T(8,128)S(1)}, f32[512,512]{1,0:T(8,128)S(1)}, f32[8,128]{1,0:T(8,128)S(1)}) custom-call(f32[512,512]{1,0:T(8,128)S(1)} %get-tuple-element.224.refs_0_.refs_5_, f32[64,512]{1,0:T(8,128)S(1)} %get-tuple-element.275.refs_1_, f32[96,512]{1,0:T(8,128)S(1)} %get-tuple-element.276.refs_2_, f32[1,512]{1,0:T(1,128)S(1)} %bitcast.47, ...), custom_call_target="tpu_custom_call" | custom-call | flops 10000000000 | tf_op jit(solution)/shard_map/square_grad_kernel0/pallas_call | solution.py:898
  63.2 2.2 %collective-permute-done.6.refs_1_ = f32[512,512]{1,0:T(8,128)S(1)} collective-permute-done((f32[512,512]{1,0:T(8,128)S(1)}, f32[512,512]{1,0:T(8,128)S(1)}, u32[]{:S(2)}, u32[]{:S(2)}) %collective-permute-start.6) | collective-permute-done | bytes 1048608 | tf_op jit(solution)/shard_map/ppermute | solution.py:933
  66.8 6.0 %pairs_grad_kernel1.1 = (f32[512,256]{1,0:T(8,128)S(1)}, f32[512,256]{1,0:T(8,128)S(1)}, f32[512,256]{1,0:T(8,128)S(1)}, f32[160,256]{1,0:T(8,128)S(1)}, f32[160,256]{1,0:T(8,128)S(1)}, /*index=5*/f32[8,128]{1,0:T(8,128)S(1)}) custom-call(f32[512,512]{1,0:T(8,128)S(1)} %get-tuple-element.231.refs_0_, f32[512,512]{1,0:T(8,128)S(1)} %get-tuple-element.232.refs_1_, ...), custom_call_target="tpu_custom_call" | custom-call | flops 10000000000 | tf_op jit(solution)/shard_map/pairs_grad_kernel1/pallas_call | solution.py:898
  76.2 3.7 %rows_grad_kernel.1 = (f32[16,512]{1,0:T(8,128)S(1)}, f32[512,512]{1,0:T(8,128)S(1)}, f32[2,16,512]{2,1,0:T(8,128)S(1)}, f32[2,16,512]{2,1,0:T(8,128)S(1)}, f32[...) custom-call(f32[512,512]{1,0:T(8,128)S(1)} %get-tuple-element.224.refs_0_.r, ...), custom_call_target="tpu_custom_call" | custom-call | flops 10000000000 | tf_op jit(solution)/shard_map/rows_grad_kernel/pallas_call | solution.py:898
  80.6 4.8 %collective-permute-start.10 = (f32[2,16,512]{2,1,0:T(8,128)S(1)}, f32[2,16,512]{2,1,0:T(8,128)S(1)}, u32[]{:S(2)}, u32[]{:S(2)}) collective-permute-start(f32[2,16,512]{2,1,0:T(8,128)S(1)} %get-tuple-element.315), channel_id=1, source_target_pairs={{0,4},{1,5},{2,6},{3,7},{4,0},{5,1},{6,2},{7,3},{8,12},{9,13},{10,... | collective-permute-start | bytes 196616 | tf_op jit(solution)/shard_map/ppermute | solution.py:1197
  85.8 2.6 %collective-permute-start.14 = (f32[128,512]{1,0:T(8,128)S(1)}, f32[128,512]{1,0:T(8,128)S(1)}, u32[]{:S(2)}, u32[]{:S(2)}) collective-permute-start(f32[128,512]{1,0:T(8,128)S(1)} %get-tuple-element.327), channel_id=1, source_target_pairs={{0,1},{1,0},{2,3},{3,2},{4,5},{5,4},{6,7},{7,6},{8,24},{9,25},{10,... | collective-permute-start | bytes 786440 | tf_op jit(solution)/shard_map/ppermute | solution.py:933
  88.4 2.1 %square_grad_kernel1.1 = (f32[512,512]{1,0:T(8,128)S(1)}, f32[512,512]{1,0:T(8,128)S(1)}, f32[8,128]{1,0:T(8,128)S(1)}) custom-call(f32[512,512]{1,0:T(8,128)S(1)} %get-tuple-element.224.refs_0_.refs_5_, f32[64,512]{1,0:T(8,128)S(1)} %get-tuple-element.275.refs_1_, f32[96,512]{1,0:T(8,128)S(1)} %get-tuple-element.276.refs_2_, f32[1,512]{1,0:T(1,128)S(1)} %bitcast.48, ...), custom_call_target="tpu_custom_call" | custom-call | flops 10000000000 | tf_op jit(solution)/shard_map/square_grad_kernel1/pallas_call | solution.py:898
  90.5 2.5 %collective-permute-start.17 = (f32[256,512]{1,0:T(8,128)S(1)}, f32[256,512]{1,0:T(8,128)S(1)}, u32[]{:S(2)}, u32[]{:S(2)}) collective-permute-start(f32[256,512]{1,0:T(8,128)S(1)} %get-tuple-element.338), channel_id=1, source_target_pairs={{0,16},{1,17},{2,18},{3,19},{4,20},{5,21},{6,22},{7,23},{8,9},{9,8... | collective-permute-start | bytes 1572872 | tf_op jit(solution)/shard_map/ppermute | solution.py:933
  93.0 2.5 %collective-permute-done.14.refs_1_ = f32[128,512]{1,0:T(8,128)S(1)} collective-permute-done((f32[128,512]{1,0:T(8,128)S(1)}, f32[128,512]{1,0:T(8,128)S(1)}, u32[]{:S(2)}, u32[]{:S(2)}) %collective-permute-start.14) | collective-permute-done | bytes 262176 | tf_op jit(solution)/shard_map/ppermute | solution.py:933
  103.3 2.1 %collective-permute-start.25 = (f32[128,512]{1,0:T(8,128)S(1)}, f32[128,512]{1,0:T(8,128)S(1)}, u32[]{:S(2)}, u32[]{:S(2)}) collective-permute-start(f32[128,512]{1,0:T(8,128)S(1)} %get-tuple-element.362.refs_0_), channel_id=1, source_target_pairs={{0,2},{1,3},{2,0},{3,1},{4,6},{5,7},{6,4},{7,5},{8,10},{9,11},{10,... | collective-permute-start | bytes 786440 | tf_op jit(solution)/shard_map/ppermute | solution.py:933
  105.4 2.6 %collective-permute-start.22 = (f32[272,512]{1,0:T(8,128)S(1)}, f32[272,512]{1,0:T(8,128)S(1)}, u32[]{:S(2)}, u32[]{:S(2)}) collective-permute-start(f32[272,512]{1,0:T(8,128)S(1)} %get-tuple-element.356), channel_id=1, source_target_pairs={{0,16},{1,17},{2,18},{3,19},{4,20},{5,21},{6,22},{7,23},{8,9},{9,8... | collective-permute-start | bytes 1671176 | tf_op jit(solution)/shard_map/ppermute | solution.py:933
  108.0 3.4 %collective-permute-start.21 = (f32[64,512]{1,0:T(8,128)S(1)}, f32[64,512]{1,0:T(8,128)S(1)}, u32[]{:S(2)}, u32[]{:S(2)}) collective-permute-start(f32[64,512]{1,0:T(8,128)S(1)} %get-tuple-element.354), channel_id=1, source_target_pairs={{0,2},{1,3},{2,0},{3,1},{4,6},{5,7},{6,4},{7,5},{8,10},{9,11},{10,... | collective-permute-start | bytes 393224 | tf_op jit(solution)/shard_map/ppermute | solution.py:933
  111.4 4.1 %collective-permute-done.22.refs_1_ = f32[272,512]{1,0:T(8,128)S(1)} collective-permute-done((f32[272,512]{1,0:T(8,128)S(1)}, f32[272,512]{1,0:T(8,128)S(1)}, u32[]{:S(2)}, u32[]{:S(2)}) %collective-permute-start.22) | collective-permute-done | bytes 557088 | tf_op jit(solution)/shard_map/ppermute | solution.py:933
  118.7 3.6 %collective-permute-done.23.refs_1_ = f32[144,512]{1,0:T(8,128)S(1)} collective-permute-done((f32[144,512]{1,0:T(8,128)S(1)}, f32[144,512]{1,0:T(8,128)S(1)}, u32[]{:S(2)}, u32[]{:S(2)}) %collective-permute-start.23) | collective-permute-done | bytes 294944 | tf_op jit(solution)/shard_map/ppermute | solution.py:933
  127.3 4.6 %collective-permute-done.26.refs_1_ = f32[64,512]{1,0:T(8,128)S(1)} collective-permute-done((f32[64,512]{1,0:T(8,128)S(1)}, f32[64,512]{1,0:T(8,128)S(1)}, u32[]{:S(2)}, u32[]{:S(2)}) %collective-permute-start.26) | collective-permute-done | bytes 131104 | tf_op jit(solution)/shard_map/ppermute | solution.py:933
  133.7 2.4 %collective-permute-start.29 = (f32[80,512]{1,0:T(8,128)S(1)}, f32[80,512]{1,0:T(8,128)S(1)}, u32[]{:S(2)}, u32[]{:S(2)}) collective-permute-start(f32[80,512]{1,0:T(8,128)S(1)} %get-tuple-element.378), channel_id=1, source_target_pairs={{0,4},{1,5},{2,6},{3,7},{4,0},{5,1},{6,2},{7,3},{8,12},{9,13},{10,... | collective-permute-start | bytes 491528 | tf_op jit(solution)/shard_map/ppermute | solution.py:933
  138.0 5.5 %collective-permute-done.32.refs_1_ = f32[128,512]{1,0:T(8,128)S(1)} collective-permute-done((f32[128,512]{1,0:T(8,128)S(1)}, f32[128,512]{1,0:T(8,128)S(1)}, u32[]{:S(2)}, u32[]{:S(2)}) %collective-permute-start.32) | collective-permute-done | bytes 262176 | tf_op jit(solution)/shard_map/ppermute | solution.py:933
  151.4 10.8 %collective-permute-done.36.refs_1_ = f32[512,512]{1,0:T(8,128)S(1)} collective-permute-done((f32[512,512]{1,0:T(8,128)S(1)}, f32[512,512]{1,0:T(8,128)S(1)}, u32[]{:S(2)}, u32[]{:S(2)}) %collective-permute-start.36) | collective-permute-done | bytes 1048608 | tf_op jit(solution)/shard_map/ppermute | solution.py:933
  164.6 3.3 %collective-permute-done.40.refs_1_ = f32[256,512]{1,0:T(8,128)S(1)} collective-permute-done((f32[256,512]{1,0:T(8,128)S(1)}, f32[256,512]{1,0:T(8,128)S(1)}, u32[]{:S(2)}, u32[]{:S(2)}) %collective-permute-start.40) | collective-permute-done | bytes 524320 | tf_op jit(solution)/shard_map/ppermute | solution.py:933
  168.0 2.9 %collective-permute-done.39.refs_1_ = f32[512,512]{1,0:T(8,128)S(1)} collective-permute-done((f32[512,512]{1,0:T(8,128)S(1)}, f32[512,512]{1,0:T(8,128)S(1)}, u32[]{:S(2)}, u32[]{:S(2)}) %collective-permute-start.39) | collective-permute-done | bytes 1048608 | tf_op jit(solution)/shard_map/ppermute | solution.py:933
  (161 shorter events, 54.6 us)
Async XLA Ops:
  2.4 7.1 %collective-permute-start = (f32[2,32,512]{2,1,0:T(8,128)S(1)}, f32[2,32,512]{2,1,0:T(8,128)S(1)}, u32[]{:S(2)}, u32[]{:S(2)}) collective-permute-start(f32[2,32,512]{2,1,0:T(8,128)S(1)} %get-tuple-element.223.refs_0_), channel_id=1, source_target_pairs={{0,1},{1,0},{2,3},{3,2},{4,5},{5,4},{6,7},{7,6},{8,9},{9,8},{10,11... | collective-permute-start | bytes 393224 | tf_op jit(solution)/shard_map/ppermute | solution.py:1052
  29.2 11.6 %collective-permute-start.4 = (f32[1024,512]{1,0:T(8,128)S(1)}, f32[1024,512]{1,0:T(8,128)S(1)}, u32[]{:S(2)}, u32[]{:S(2)}) collective-permute-start(f32[1024,512]{1,0:T(8,128)S(1)} %get-tuple-element.261), channel_id=1, source_target_pairs={{0,8},{1,9},{2,10},{3,11},{4,12},{5,13},{6,14},{7,15},{8,0},{9,1},... | collective-permute-start | bytes 6291464 | tf_op jit(solution)/shard_map/ppermute | solution.py:933
  40.3 10.0 %collective-permute-start.5 = (f32[1024,512]{1,0:T(8,128)S(1)}, f32[1024,512]{1,0:T(8,128)S(1)}, u32[]{:S(2)}, u32[]{:S(2)}) collective-permute-start(f32[1024,512]{1,0:T(8,128)S(1)} %get-tuple-element.271), channel_id=1, source_target_pairs={{0,8},{1,9},{2,10},{3,11},{4,12},{5,13},{6,14},{7,15},{8,0},{9,1},... | collective-permute-start | bytes 6291464 | tf_op jit(solution)/shard_map/ppermute | solution.py:933
  41.1 31.7 %collective-permute-start.8 = (f32[512,512]{1,0:T(8,128)S(1)}, f32[512,512]{1,0:T(8,128)S(1)}, u32[]{:S(2)}, u32[]{:S(2)}) collective-permute-start(f32[512,512]{1,0:T(8,128)S(1)} %get-tuple-element.309), channel_id=1, source_target_pairs={{0,2},{1,3},{2,0},{3,1},{4,6},{5,7},{6,4},{7,5},{8,10},{9,11},{10,... | collective-permute-start | bytes 3145736 | tf_op jit(solution)/shard_map/ppermute | solution.py:933
  50.5 14.9 %collective-permute-start.6 = (f32[512,512]{1,0:T(8,128)S(1)}, f32[512,512]{1,0:T(8,128)S(1)}, u32[]{:S(2)}, u32[]{:S(2)}) collective-permute-start(f32[512,512]{1,0:T(8,128)S(1)} %get-tuple-element.293), channel_id=1, source_target_pairs={{0,16},{1,17},{2,18},{3,19},{4,20},{5,21},{6,22},{7,23},{8,9},{9,8... | collective-permute-start | bytes 3145736 | tf_op jit(solution)/shard_map/ppermute | solution.py:933
  63.1 22.4 %collective-permute-start.12 = (f32[512,512]{1,0:T(8,128)S(1)}, f32[512,512]{1,0:T(8,128)S(1)}, u32[]{:S(2)}, u32[]{:S(2)}) collective-permute-start(f32[512,512]{1,0:T(8,128)S(1)} %get-tuple-element.320), channel_id=1, source_target_pairs={{0,8},{1,9},{2,10},{3,11},{4,12},{5,13},{6,14},{7,15},{8,0},{9,1},... | collective-permute-start | bytes 3145736 | tf_op jit(solution)/shard_map/ppermute | solution.py:933
  65.5 9.5 %collective-permute-start.7 = (f32[256,512]{1,0:T(8,128)S(1)}, f32[256,512]{1,0:T(8,128)S(1)}, u32[]{:S(2)}, u32[]{:S(2)}) collective-permute-start(f32[256,512]{1,0:T(8,128)S(1)} %get-tuple-element.307), channel_id=1, source_target_pairs={{0,1},{1,0},{2,3},{3,2},{4,5},{5,4},{6,7},{7,6},{8,24},{9,25},{10,... | collective-permute-start | bytes 1572872 | tf_op jit(solution)/shard_map/ppermute | solution.py:933
  72.9 12.8 %collective-permute-start.11 = (f32[256,512]{1,0:T(8,128)S(1)}, f32[256,512]{1,0:T(8,128)S(1)}, u32[]{:S(2)}, u32[]{:S(2)}) collective-permute-start(f32[256,512]{1,0:T(8,128)S(1)} %get-tuple-element.318), channel_id=1, source_target_pairs={{0,16},{1,17},{2,18},{3,19},{4,20},{5,21},{6,22},{7,23},{8,9},{9,8... | collective-permute-start | bytes 1572872 | tf_op jit(solution)/shard_map/ppermute | solution.py:933
  75.0 10.4 %collective-permute-start.13 = (f32[128,512]{1,0:T(8,128)S(1)}, f32[128,512]{1,0:T(8,128)S(1)}, u32[]{:S(2)}, u32[]{:S(2)}) collective-permute-start(f32[128,512]{1,0:T(8,128)S(1)} %get-tuple-element.322), channel_id=1, source_target_pairs={{0,2},{1,3},{2,0},{3,1},{4,6},{5,7},{6,4},{7,5},{8,10},{9,11},{10,... | collective-permute-start | bytes 786440 | tf_op jit(solution)/shard_map/ppermute | solution.py:933
  79.9 15.6 %collective-permute-start.9 = (f32[2,16,512]{2,1,0:T(8,128)S(1)}, f32[2,16,512]{2,1,0:T(8,128)S(1)}, u32[]{:S(2)}, u32[]{:S(2)}) collective-permute-start(f32[2,16,512]{2,1,0:T(8,128)S(1)} %get-tuple-element.314), channel_id=1, source_target_pairs={{1,2},{2,1},{3,4},{4,3},{5,6},{6,5},{9,10},{10,9},{11,12},{12,11},... | collective-permute-start | bytes 196616 | tf_op jit(solution)/shard_map/ppermute | solution.py:1194
  80.6 15.4 %collective-permute-start.10 = (f32[2,16,512]{2,1,0:T(8,128)S(1)}, f32[2,16,512]{2,1,0:T(8,128)S(1)}, u32[]{:S(2)}, u32[]{:S(2)}) collective-permute-start(f32[2,16,512]{2,1,0:T(8,128)S(1)} %get-tuple-element.315), channel_id=1, source_target_pairs={{0,4},{1,5},{2,6},{3,7},{4,0},{5,1},{6,2},{7,3},{8,12},{9,13},{10,... | collective-permute-start | bytes 196616 | tf_op jit(solution)/shard_map/ppermute | solution.py:1197
  85.5 15.9 %collective-permute-start.16 = (f32[128,512]{1,0:T(8,128)S(1)}, f32[128,512]{1,0:T(8,128)S(1)}, u32[]{:S(2)}, u32[]{:S(2)}) collective-permute-start(f32[128,512]{1,0:T(8,128)S(1)} %get-tuple-element.336), channel_id=1, source_target_pairs={{0,4},{1,5},{2,6},{3,7},{4,0},{5,1},{6,2},{7,3},{8,12},{9,13},{10,... | collective-permute-start | bytes 786440 | tf_op jit(solution)/shard_map/ppermute | solution.py:933
  85.8 9.8 %collective-permute-start.14 = (f32[128,512]{1,0:T(8,128)S(1)}, f32[128,512]{1,0:T(8,128)S(1)}, u32[]{:S(2)}, u32[]{:S(2)}) collective-permute-start(f32[128,512]{1,0:T(8,128)S(1)} %get-tuple-element.327), channel_id=1, source_target_pairs={{0,1},{1,0},{2,3},{3,2},{4,5},{5,4},{6,7},{7,6},{8,24},{9,25},{10,... | collective-permute-start | bytes 786440 | tf_op jit(solution)/shard_map/ppermute | solution.py:933
  90.5 9.8 %collective-permute-start.17 = (f32[256,512]{1,0:T(8,128)S(1)}, f32[256,512]{1,0:T(8,128)S(1)}, u32[]{:S(2)}, u32[]{:S(2)}) collective-permute-start(f32[256,512]{1,0:T(8,128)S(1)} %get-tuple-element.338), channel_id=1, source_target_pairs={{0,16},{1,17},{2,18},{3,19},{4,20},{5,21},{6,22},{7,23},{8,9},{9,8... | collective-permute-start | bytes 1572872 | tf_op jit(solution)/shard_map/ppermute | solution.py:933
  98.2 18.4 %collective-permute-start.24 = (f32[128,512]{1,0:T(8,128)S(1)}, f32[128,512]{1,0:T(8,128)S(1)}, u32[]{:S(2)}, u32[]{:S(2)}) collective-permute-start(f32[128,512]{1,0:T(8,128)S(1)} %get-tuple-element.361), channel_id=1, source_target_pairs={{0,4},{1,5},{2,6},{3,7},{4,0},{5,1},{6,2},{7,3},{8,12},{9,13},{10,... | collective-permute-start | bytes 786440 | tf_op jit(solution)/shard_map/ppermute | solution.py:933
  100.4 7.6 %collective-permute-start.20 = (f32[128,512]{1,0:T(8,128)S(1)}, f32[128,512]{1,0:T(8,128)S(1)}, u32[]{:S(2)}, u32[]{:S(2)}) collective-permute-start(f32[128,512]{1,0:T(8,128)S(1)} %get-tuple-element.351), channel_id=1, source_target_pairs={{0,1},{1,0},{2,3},{3,2},{4,5},{5,4},{6,7},{7,6},{8,24},{9,25},{10,... | collective-permute-start | bytes 786440 | tf_op jit(solution)/shard_map/ppermute | solution.py:933
  101.6 30.3 %collective-permute-start.19 = (f32[2,32,512]{2,1,0:T(8,128)S(1)}, f32[2,32,512]{2,1,0:T(8,128)S(1)}, u32[]{:S(2)}, u32[]{:S(2)}) collective-permute-start(f32[2,32,512]{2,1,0:T(8,128)S(1)} %get-tuple-element.346), channel_id=1, source_target_pairs={{0,1},{1,0},{2,3},{3,2},{4,5},{5,4},{6,7},{7,6},{8,9},{9,8},{10,11... | collective-permute-start | bytes 393224 | tf_op jit(solution)/shard_map/ppermute | solution.py:1216
  103.3 13.2 %collective-permute-start.25 = (f32[128,512]{1,0:T(8,128)S(1)}, f32[128,512]{1,0:T(8,128)S(1)}, u32[]{:S(2)}, u32[]{:S(2)}) collective-permute-start(f32[128,512]{1,0:T(8,128)S(1)} %get-tuple-element.362.refs_0_), channel_id=1, source_target_pairs={{0,2},{1,3},{2,0},{3,1},{4,6},{5,7},{6,4},{7,5},{8,10},{9,11},{10,... | collective-permute-start | bytes 786440 | tf_op jit(solution)/shard_map/ppermute | solution.py:933
  105.4 10.1 %collective-permute-start.22 = (f32[272,512]{1,0:T(8,128)S(1)}, f32[272,512]{1,0:T(8,128)S(1)}, u32[]{:S(2)}, u32[]{:S(2)}) collective-permute-start(f32[272,512]{1,0:T(8,128)S(1)} %get-tuple-element.356), channel_id=1, source_target_pairs={{0,16},{1,17},{2,18},{3,19},{4,20},{5,21},{6,22},{7,23},{8,9},{9,8... | collective-permute-start | bytes 1671176 | tf_op jit(solution)/shard_map/ppermute | solution.py:933
  108.0 14.3 %collective-permute-start.21 = (f32[64,512]{1,0:T(8,128)S(1)}, f32[64,512]{1,0:T(8,128)S(1)}, u32[]{:S(2)}, u32[]{:S(2)}) collective-permute-start(f32[64,512]{1,0:T(8,128)S(1)} %get-tuple-element.354), channel_id=1, source_target_pairs={{0,2},{1,3},{2,0},{3,1},{4,6},{5,7},{6,4},{7,5},{8,10},{9,11},{10,... | collective-permute-start | bytes 393224 | tf_op jit(solution)/shard_map/ppermute | solution.py:933
  116.6 8.5 %collective-permute-start.27 = (f32[128,512]{1,0:T(8,128)S(1)}, f32[128,512]{1,0:T(8,128)S(1)}, u32[]{:S(2)}, u32[]{:S(2)}) collective-permute-start(f32[128,512]{1,0:T(8,128)S(1)} %get-tuple-element.369.refs_0_), channel_id=1, source_target_pairs={{0,1},{1,0},{2,3},{3,2},{4,5},{5,4},{6,7},{7,6},{8,24},{9,25},{10,... | collective-permute-start | bytes 786440 | tf_op jit(solution)/shard_map/ppermute | solution.py:933
  117.9 20.1 %collective-permute-start.33 = (f32[256,512]{1,0:T(8,128)S(1)}, f32[256,512]{1,0:T(8,128)S(1)}, u32[]{:S(2)}, u32[]{:S(2)}) collective-permute-start(f32[256,512]{1,0:T(8,128)S(1)} %get-tuple-element.384.refs_0_), channel_id=1, source_target_pairs={{0,1},{1,0},{2,3},{3,2},{4,5},{5,4},{6,7},{7,6},{8,24},{9,25},{10,... | collective-permute-start | bytes 1572872 | tf_op jit(solution)/shard_map/ppermute | solution.py:933
  122.4 9.5 %collective-permute-start.26 = (f32[64,512]{1,0:T(8,128)S(1)}, f32[64,512]{1,0:T(8,128)S(1)}, u32[]{:S(2)}, u32[]{:S(2)}) collective-permute-start(f32[64,512]{1,0:T(8,128)S(1)} %get-tuple-element.368), channel_id=1, source_target_pairs={{0,4},{1,5},{2,6},{3,7},{4,0},{5,1},{6,2},{7,3},{8,12},{9,13},{10,... | collective-permute-start | bytes 393224 | tf_op jit(solution)/shard_map/ppermute | solution.py:933
  123.0 10.7 %collective-permute-start.28 = (f32[80,512]{1,0:T(8,128)S(1)}, f32[80,512]{1,0:T(8,128)S(1)}, u32[]{:S(2)}, u32[]{:S(2)}) collective-permute-start(f32[80,512]{1,0:T(8,128)S(1)} %get-tuple-element.375), channel_id=1, source_target_pairs={{0,2},{1,3},{2,0},{3,1},{4,6},{5,7},{6,4},{7,5},{8,10},{9,11},{10,... | collective-permute-start | bytes 491528 | tf_op jit(solution)/shard_map/ppermute | solution.py:933
  125.2 11.2 %collective-permute-start.31 = (f32[256,512]{1,0:T(8,128)S(1)}, f32[256,512]{1,0:T(8,128)S(1)}, u32[]{:S(2)}, u32[]{:S(2)}) collective-permute-start(f32[256,512]{1,0:T(8,128)S(1)} %get-tuple-element.380.refs_0_), channel_id=1, source_target_pairs={{0,16},{1,17},{2,18},{3,19},{4,20},{5,21},{6,22},{7,23},{8,9},{9,8... | collective-permute-start | bytes 1572872 | tf_op jit(solution)/shard_map/ppermute | solution.py:933
  133.7 10.4 %collective-permute-start.29 = (f32[80,512]{1,0:T(8,128)S(1)}, f32[80,512]{1,0:T(8,128)S(1)}, u32[]{:S(2)}, u32[]{:S(2)}) collective-permute-start(f32[80,512]{1,0:T(8,128)S(1)} %get-tuple-element.378), channel_id=1, source_target_pairs={{0,4},{1,5},{2,6},{3,7},{4,0},{5,1},{6,2},{7,3},{8,12},{9,13},{10,... | collective-permute-start | bytes 491528 | tf_op jit(solution)/shard_map/ppermute | solution.py:933
  144.6 17.6 %collective-permute-start.36 = (f32[512,512]{1,0:T(8,128)S(1)}, f32[512,512]{1,0:T(8,128)S(1)}, u32[]{:S(2)}, u32[]{:S(2)}) collective-permute-start(f32[512,512]{1,0:T(8,128)S(1)} %get-tuple-element.391.refs_0_), channel_id=1, source_target_pairs={{0,16},{1,17},{2,18},{3,19},{4,20},{5,21},{6,22},{7,23},{8,9},{9,8... | collective-permute-start | bytes 3145736 | tf_op jit(solution)/shard_map/ppermute | solution.py:933
  146.6 24.3 %collective-permute-start.39 = (f32[512,512]{1,0:T(8,128)S(1)}, f32[512,512]{1,0:T(8,128)S(1)}, u32[]{:S(2)}, u32[]{:S(2)}) collective-permute-start(f32[512,512]{1,0:T(8,128)S(1)} %get-tuple-element.397.refs_0_), channel_id=1, source_target_pairs={{0,2},{1,3},{2,0},{3,1},{4,6},{5,7},{6,4},{7,5},{8,10},{9,11},{10,... | collective-permute-start | bytes 3145736 | tf_op jit(solution)/shard_map/ppermute | solution.py:933
  148.5 19.3 %collective-permute-start.40 = (f32[256,512]{1,0:T(8,128)S(1)}, f32[256,512]{1,0:T(8,128)S(1)}, u32[]{:S(2)}, u32[]{:S(2)}) collective-permute-start(f32[256,512]{1,0:T(8,128)S(1)} %get-tuple-element.398.refs_0_), channel_id=1, source_target_pairs={{0,16},{1,17},{2,18},{3,19},{4,20},{5,21},{6,22},{7,23},{8,9},{9,8... | collective-permute-start | bytes 1572872 | tf_op jit(solution)/shard_map/ppermute | solution.py:933
  150.6 11.9 %collective-permute-start.35 = (f32[128,512]{1,0:T(8,128)S(1)}, f32[128,512]{1,0:T(8,128)S(1)}, u32[]{:S(2)}, u32[]{:S(2)}) collective-permute-start(f32[128,512]{1,0:T(8,128)S(1)} %get-tuple-element.390.refs_0_), channel_id=1, source_target_pairs={{0,1},{1,0},{2,3},{3,2},{4,5},{5,4},{6,7},{7,6},{8,24},{9,25},{10,... | collective-permute-start | bytes 786440 | tf_op jit(solution)/shard_map/ppermute | solution.py:933
  162.4 8.7 %collective-permute-start.38 = (f32[1024,512]{1,0:T(8,128)S(1)}, f32[1024,512]{1,0:T(8,128)S(1)}, u32[]{:S(2)}, u32[]{:S(2)}) collective-permute-start(f32[1024,512]{1,0:T(8,128)S(1)} %get-tuple-element.396.refs_0_), channel_id=1, source_target_pairs={{0,8},{1,9},{2,10},{3,11},{4,12},{5,13},{6,14},{7,15},{8,0},{9,1},... | collective-permute-start | bytes 6291464 | tf_op jit(solution)/shard_map/ppermute | solution.py:933
  162.5 10.9 %collective-permute-start.37 = (f32[256,512]{1,0:T(8,128)S(1)}, f32[256,512]{1,0:T(8,128)S(1)}, u32[]{:S(2)}, u32[]{:S(2)}) collective-permute-start(f32[256,512]{1,0:T(8,128)S(1)} %get-tuple-element.394.refs_0_), channel_id=1, source_target_pairs={{0,16},{1,17},{2,18},{3,19},{4,20},{5,21},{6,22},{7,23},{8,9},{9,8... | collective-permute-start | bytes 1572872 | tf_op jit(solution)/shard_map/ppermute | solution.py:933
  (36 other events, 150.7 us)
